TPU v7x, 32 devices: a whole 2x2x4 slice. The times are simulated.
32 devices in a mesh: items: 4 (over y, x), rows: 8 (over z, core).
Axes of the slice: x: 2, y: 2, z: 4, core: 2. Of those that a mesh axis runs over, the one named last changes fastest.
Arguments:
- image: bfloat16 [4, 64, 64, 512], P('items', 'rows'), may hold values from -18 to 18
- embed: bfloat16 [4, 2048], P('items'), may hold values from -6 to 6
- text: bfloat16 [4, 128, 2048], P('items', 'rows'), may hold values from -6 to 6
- extent: int32 [4, 2], P('items'), may hold values from 32 to 64, as said below
- first_norm_gain1: float32 [512], replicated, may hold values from 0.1 to 1.9
- conv1_w: bfloat16 [3, 3, 512, 512], replicated, may hold values from -0.09375 to 0.09375
- embed_w: bfloat16 [2048, 1024], replicated, may hold values from -0.125 to 0.125
- second_norm_gain2: float32 [512], replicated, may hold values from 0.1 to 1.9
- conv2_w: bfloat16 [3, 3, 512, 512], replicated, may hold values from -0.09375 to 0.09375
- attention_norm_gain: float32 [512], replicated, may hold values from 0.1 to 1.9
- qkv_w: bfloat16 [512, 1536], replicated, may hold values from -0.25 to 0.25
- text_w: bfloat16 [2048, 1024], replicated, may hold values from -0.125 to 0.125
- proj_w: bfloat16 [512, 512], replicated, may hold values from -6 to 6
- cotangent: bfloat16 [4, 64, 64, 512], P('items', 'rows'), may hold values from -6 to 6
Outputs:
- output: bfloat16 [4, 64, 64, 512], P('items', 'rows')
- image_grad: float32 [4, 64, 64, 512], P('items', 'rows')
- embed_grad: float32 [4, 2048], P('items')
- text_grad: float32 [4, 128, 2048], P('items', 'rows')
- norm1_gain_grad: float32 [512], P('rows')
- conv1_w_grad: float32 [3, 3, 512, 512], P(None, None, None, 'rows')
- embed_w_grad: float32 [2048, 1024], P('rows')
- norm2_gain_grad: float32 [512], P('rows')
- conv2_w_grad: float32 [3, 3, 512, 512], P(None, None, None, 'rows')
- attn_gain_grad: float32 [512], P('rows')
- qkv_w_grad: float32 [512, 1536], P(None, 'rows')
- text_w_grad: float32 [2048, 1024], P('rows')
- proj_w_grad: float32 [512, 512], P(None, 'rows')
Inputs may be any that keep to these rules, and one draw needn't show every extreme that they name: `extent`: each image's valid rows and columns are 64 and 64 minus the same multiple 0, 1 or 2 of a quarter of them; in every draw some image fills its frame and some other image keeps half of its rows and half of its columns.
All inputs are finite; a program needn't handle non-finite values.
Results may differ from a plain program's by a relative error of at most 0.018.
Values may be sent and summed in bfloat16 or wider, within the bound.
A program may use at most 192 MiB of HBM per device.

v0:
```python
import jax
import jax.numpy as jnp
from jax import lax
from jax.sharding import PartitionSpec as P

GROUPS = 32
HEADS = 8


eps = 1e-05
negative = -1e30


def padded_2(shard, sides, width):
    for axis, dim in sides:
        count, length = (lax.axis_size(axis), shard.shape[dim])
        up = [(i, (i + 1) % count) for i in range(count - 1)]
        down = [(j, i) for i, j in up]
        last = lax.slice_in_dim(shard, length - width, length, axis=dim)
        first = lax.slice_in_dim(shard, 0, width, axis=dim)
        before = lax.ppermute(last, axis, up)
        after = lax.ppermute(first, axis, down)
        shard = jnp.concatenate([before, shard, after], axis=dim)
    return shard


def framed(values):
    padded = padded_2(values, (("rows", 1),), 1)
    return jnp.pad(padded, ((0, 0), (0, 0), (1, 1), (0, 0)))


def conv_apply(padded, kernel, layout):
    return lax.conv_general_dilated(
        padded,
        kernel,
        (1, 1),
        ((0, 0), (0, 0)),
        dimension_numbers=("NHWC", layout, "NHWC"),
        preferred_element_type=jnp.float32,
    )


def kernel_grad(padded, grad_out):
    rows_dev, width = (grad_out.shape[1], grad_out.shape[2])
    taps = []
    for tap_row in range(3):
        for tap_col in range(3):
            shifted = padded[:, tap_row : tap_row + rows_dev, tap_col : tap_col + width]
            taps.append(
                jnp.einsum("irwc,irwk->ck", shifted, grad_out, preferred_element_type=jnp.float32)
            )
    return jnp.stack(taps).reshape(3, 3, padded.shape[3], grad_out.shape[3])


def silu_slope(values):
    sigmoid = jax.nn.sigmoid(values)
    return sigmoid * (1.0 + values * (1.0 - sigmoid))


def grouped_input(values):
    return values.reshape(values.shape[:3] + (GROUPS, values.shape[3] // GROUPS))


def group_norm_forward(values, group_counts, image_window):
    shaped = grouped_input(values)
    sums, squares = lax.psum(
        (jnp.sum(shaped, axis=(1, 2, 4)), jnp.sum(shaped * shaped, axis=(1, 2, 4))), "rows"
    )
    average = sums / group_counts[:, None]
    inverse_deviation = lax.rsqrt(squares / group_counts[:, None] - average * average + eps)
    normal = (shaped - average[:, None, None, :, None]) * inverse_deviation[:, None, None, :, None]
    return (normal.reshape(values.shape) * image_window, inverse_deviation)


def apply_group_norm(
    normalized_gradient,
    normalized_input,
    inverse_deviation,
    gradient_total_sum,
    cross_product_sum,
    group_counts,
    image_window,
):
    shaped_grad = grouped_input(normalized_gradient)
    reshaped_input = grouped_input(normalized_input)
    mean_grad = (gradient_total_sum / group_counts[:, None])[:, None, None, :, None]
    mean_cross = (cross_product_sum / group_counts[:, None])[:, None, None, :, None]
    result = (shaped_grad - mean_grad - reshaped_input * mean_cross) * inverse_deviation[
        :, None, None, :, None
    ]
    return result.reshape(normalized_gradient.shape) * image_window


def group_norm_backward(
    norm_gradient, normalized_input, inverse_deviation, norm_gain, group_counts, image_window
):
    normalized_gradient = norm_gradient * norm_gain
    shaped_grad = grouped_input(normalized_gradient)
    reshaped_input = grouped_input(normalized_input)
    gradient_total_sum, cross_product_sum = lax.psum(
        (
            jnp.sum(shaped_grad, axis=(1, 2, 4)),
            jnp.sum(shaped_grad * reshaped_input, axis=(1, 2, 4)),
        ),
        "rows",
    )
    correction_term = apply_group_norm(
        normalized_gradient,
        normalized_input,
        inverse_deviation,
        gradient_total_sum,
        cross_product_sum,
        group_counts,
        image_window,
    )
    return (correction_term, jnp.sum(norm_gradient * normalized_input, axis=(0, 1, 2)))


def shards(
    image,
    embed,
    text,
    extent,
    first_norm_gain1,
    conv1_w,
    embed_w,
    second_norm_gain2,
    conv2_w,
    attention_norm_gain,
    qkv_w,
    text_w,
    proj_w,
    cotangent,
):
    images, rows_dev, width, channels = image.shape
    parts = lax.axis_size("rows")
    pairs = images * HEADS // parts
    head_dim = channels // HEADS
    first_row = lax.axis_index("rows") * rows_dev
    rowpos = first_row + jnp.arange(rows_dev, dtype=jnp.int32)
    colpos = jnp.arange(width, dtype=jnp.int32)
    inside = (
        (rowpos[None, :, None] < extent[:, 0, None, None])
        & (colpos[None, None, :] < extent[:, 1, None, None])
    ).astype(jnp.float32)
    image_window = inside[..., None]
    group_counts = (extent[:, 0] * extent[:, 1]).astype(jnp.float32) * (channels // GROUPS)
    start_index = image.astype(jnp.float32) * image_window
    first_normalized_input, first_inverse_deviation = group_norm_forward(
        start_index, group_counts, image_window
    )
    first_preactivation = first_normalized_input * first_norm_gain1
    hidden = (jax.nn.silu(first_preactivation) * image_window).astype(jnp.bfloat16)
    hidden_pad = framed(hidden)
    first_output = conv_apply(hidden_pad, conv1_w, "HWIO") * image_window
    embed_float = embed.astype(jnp.float32)
    embed_low = jax.nn.silu(embed_float).astype(jnp.bfloat16)
    shifts = jnp.dot(embed_low, embed_w, preferred_element_type=jnp.float32)
    scale = shifts[:, None, None, :channels]
    shift = shifts[:, None, None, channels:]
    second_normalized_input, second_inverse_deviation = group_norm_forward(
        first_output, group_counts, image_window
    )
    normalized_output = second_normalized_input * second_norm_gain2
    moved = normalized_output * (1.0 + scale) + shift
    second = (jax.nn.silu(moved) * image_window).astype(jnp.bfloat16)
    second_pad = framed(second)
    middle_output = start_index + conv_apply(second_pad, conv2_w, "HWIO") * image_window
    attention_normalized_input, attention_inverse_deviation = group_norm_forward(
        middle_output, group_counts, image_window
    )
    attention_input = (attention_normalized_input * attention_norm_gain).astype(jnp.bfloat16)
    qkv_shaped = qkv_w.reshape(channels, HEADS, 3 * head_dim)
    text_shaped = text_w.reshape(text_w.shape[0], HEADS, 2 * head_dim)
    proj_shaped = proj_w.reshape(HEADS, head_dim, channels)
    qkv_pix = jnp.einsum(
        "irwc,chk->ihrwk", attention_input, qkv_shaped, preferred_element_type=jnp.float32
    ).astype(jnp.bfloat16)
    text_pix = jnp.einsum(
        "itc,chk->ihtk", text, text_shaped, preferred_element_type=jnp.float32
    ).astype(jnp.bfloat16)
    qkv_pair, text_pair = (
        lax.all_to_all(
            qkv_pix.reshape((images * HEADS,) + qkv_pix.shape[2:]),
            "rows",
            split_axis=0,
            concat_axis=1,
            tiled=True,
        ),
        lax.all_to_all(
            text_pix.reshape((images * HEADS,) + text_pix.shape[2:]),
            "rows",
            split_axis=0,
            concat_axis=1,
            tiled=True,
        ),
    )
    frame_rows = qkv_pair.shape[1]
    text_len = text_pair.shape[1]
    tokens = frame_rows * width
    pair_index = lax.axis_index("rows") * pairs + jnp.arange(pairs, dtype=jnp.int32)
    pick = ((pair_index // HEADS)[:, None] == jnp.arange(images, dtype=jnp.int32)[None, :]).astype(
        jnp.int32
    )
    pair_extent = jnp.sum(pick[:, :, None] * extent[None, :, :], axis=1)
    pixel_ok = (
        jnp.arange(frame_rows, dtype=jnp.int32)[None, :, None] < pair_extent[:, 0, None, None]
    ) & (colpos[None, None, :] < pair_extent[:, 1, None, None])
    keys_ok = jnp.concatenate(
        [jnp.ones((pairs, text_len), jnp.bool_), pixel_ok.reshape(pairs, tokens)], axis=1
    )
    flat = qkv_pair.reshape(pairs, tokens, 3 * head_dim)
    queries = flat[:, :, :head_dim]
    keys = jnp.concatenate(
        [text_pair[:, :, :head_dim], flat[:, :, head_dim : 2 * head_dim]], axis=1
    )
    values = jnp.concatenate([text_pair[:, :, head_dim:], flat[:, :, 2 * head_dim :]], axis=1)
    block = min(512, tokens)
    blocks = tokens // block
    factor = head_dim ** (-0.5)

    def scores_of(index):
        query_block = lax.dynamic_slice_in_dim(queries, index * block, block, 1)
        scores = (
            jnp.einsum("pqd,pkd->pqk", query_block, keys, preferred_element_type=jnp.float32)
            * factor
        )
        return (query_block, jnp.where(keys_ok[:, None, :], scores, negative))

    def forward_block(index):
        query_block, scores = scores_of(index)
        peak = jnp.max(scores, axis=2, keepdims=True)
        raised = jnp.exp(scores - peak)
        total = jnp.sum(raised, axis=2, keepdims=True)
        attn_probs = (raised / total).astype(jnp.bfloat16)
        attended = jnp.einsum(
            "pqk,pkd->pqd", attn_probs, values, preferred_element_type=jnp.float32
        )
        return (attended.astype(jnp.bfloat16), (peak + jnp.log(total))[:, :, 0])

    attended, logsum = lax.map(forward_block, jnp.arange(blocks))
    attended = jnp.moveaxis(attended, 0, 1).reshape(pairs, frame_rows, width, head_dim)
    logsum = jnp.moveaxis(logsum, 0, 1).reshape(pairs, tokens)
    heads_out = lax.all_to_all(attended, "rows", split_axis=1, concat_axis=0, tiled=True)
    heads_out = heads_out.reshape(images, HEADS, rows_dev, width, head_dim)
    projected = jnp.einsum(
        "ihrwd,hdc->irwc", heads_out, proj_shaped, preferred_element_type=jnp.float32
    )
    output = (middle_output + projected * image_window).astype(jnp.bfloat16)
    grad_out = cotangent.astype(jnp.float32)
    grad_proj = (grad_out * image_window).astype(jnp.bfloat16)
    proj_grad = jnp.einsum(
        "ihrwd,irwc->hdc", heads_out, grad_proj, preferred_element_type=jnp.float32
    ).reshape(channels, channels)
    grad_heads = jnp.einsum(
        "irwc,hdc->ihrwd", grad_proj, proj_shaped, preferred_element_type=jnp.float32
    ).astype(jnp.bfloat16)
    grad_pair = lax.all_to_all(
        grad_heads.reshape((images * HEADS,) + grad_heads.shape[2:]),
        "rows",
        split_axis=0,
        concat_axis=1,
        tiled=True,
    )
    grad_flat = grad_pair.reshape(pairs, tokens, head_dim)

    def backward_block(carry, index):
        key_grad, value_grad = carry
        query_block, scores = scores_of(index)
        lse_block = lax.dynamic_slice_in_dim(logsum, index * block, block, 1)
        attn_probs = jnp.exp(scores - lse_block[:, :, None])
        grad_block = lax.dynamic_slice_in_dim(grad_flat, index * block, block, 1)
        grad_probs = jnp.einsum(
            "pqd,pkd->pqk", grad_block, values, preferred_element_type=jnp.float32
        )
        grad_scores = (
            attn_probs * (grad_probs - jnp.sum(grad_probs * attn_probs, axis=2, keepdims=True))
        ).astype(jnp.bfloat16)
        query_grad = (
            jnp.einsum("pqk,pkd->pqd", grad_scores, keys, preferred_element_type=jnp.float32)
            * factor
        )
        key_grad = (
            key_grad
            + jnp.einsum(
                "pqk,pqd->pkd", grad_scores, query_block, preferred_element_type=jnp.float32
            )
            * factor
        )
        value_grad = value_grad + jnp.einsum(
            "pqk,pqd->pkd",
            attn_probs.astype(jnp.bfloat16),
            grad_block,
            preferred_element_type=jnp.float32,
        )
        return ((key_grad, value_grad), query_grad)

    zeros = jnp.zeros(keys.shape, jnp.float32)
    (key_grad, value_grad), query_grad = lax.scan(
        backward_block, (zeros, zeros), jnp.arange(blocks)
    )
    query_grad = jnp.moveaxis(query_grad, 0, 1).reshape(pairs, tokens, head_dim)
    image_qkv_grad = (
        jnp.concatenate([query_grad, key_grad[:, text_len:], value_grad[:, text_len:]], axis=2)
        .astype(jnp.bfloat16)
        .reshape(pairs, frame_rows, width, 3 * head_dim)
    )
    text_kv_grad = jnp.concatenate(
        [key_grad[:, :text_len], value_grad[:, :text_len]], axis=2
    ).astype(jnp.bfloat16)
    qkv_back, text_back = (
        lax.all_to_all(image_qkv_grad, "rows", split_axis=1, concat_axis=0, tiled=True),
        lax.all_to_all(text_kv_grad, "rows", split_axis=1, concat_axis=0, tiled=True),
    )
    qkv_back = qkv_back.reshape(images, HEADS, rows_dev, width, 3 * head_dim)
    text_back = text_back.reshape(images, HEADS, text.shape[1], 2 * head_dim)
    attention_gradient = jnp.einsum(
        "ihrwk,chk->irwc", qkv_back, qkv_shaped, preferred_element_type=jnp.float32
    )
    qkv_grad = jnp.einsum(
        "irwc,ihrwk->chk", attention_input, qkv_back, preferred_element_type=jnp.float32
    ).reshape(channels, 3 * channels)
    text_grad = jnp.einsum(
        "ihtk,chk->itc", text_back, text_shaped, preferred_element_type=jnp.float32
    )
    text_w_grad = jnp.einsum(
        "itc,ihtk->chk", text, text_back, preferred_element_type=jnp.float32
    ).reshape(text_w.shape[0], 2 * channels)
    attn_term, attn_gain_grad = group_norm_backward(
        attention_gradient * image_window,
        attention_normalized_input,
        attention_inverse_deviation,
        attention_norm_gain,
        group_counts,
        image_window,
    )
    grad_middle = grad_out + attn_term
    grad_conv2 = (grad_middle * image_window).astype(jnp.bfloat16)
    conv2_grad = kernel_grad(second_pad, grad_conv2)
    grad_second = conv_apply(framed(grad_conv2), conv2_w[::-1, ::-1], "HWOI") * image_window
    grad_moved = grad_second * silu_slope(moved)
    normalized_output_gradient = grad_moved * (1.0 + scale)
    second_normalized_gradient = normalized_output_gradient * second_norm_gain2
    shaped_grad = grouped_input(second_normalized_gradient)
    reshaped_input = grouped_input(second_normalized_input)
    gradient_total_sum, cross_product_sum, scale_sum, shift_sum = lax.psum(
        (
            jnp.sum(shaped_grad, axis=(1, 2, 4)),
            jnp.sum(shaped_grad * reshaped_input, axis=(1, 2, 4)),
            jnp.sum(grad_moved * normalized_output, axis=(1, 2)),
            jnp.sum(grad_moved, axis=(1, 2)),
        ),
        "rows",
    )
    first_output_gradient = apply_group_norm(
        second_normalized_gradient,
        second_normalized_input,
        second_inverse_deviation,
        gradient_total_sum,
        cross_product_sum,
        group_counts,
        image_window,
    )
    second_norm_gradient2 = jnp.sum(
        normalized_output_gradient * second_normalized_input, axis=(0, 1, 2)
    )
    grad_shifts = jnp.concatenate([scale_sum, shift_sum], axis=1).astype(jnp.bfloat16)
    embed_grad = jnp.einsum(
        "ik,ck->ic", grad_shifts, embed_w, preferred_element_type=jnp.float32
    ) * silu_slope(embed_float)
    embed_share = embed_w.shape[0] // parts
    embed_rows = lax.dynamic_slice_in_dim(
        embed_low, lax.axis_index("rows") * embed_share, embed_share, 1
    )
    embed_w_grad = jnp.einsum(
        "ic,ik->ck", embed_rows, grad_shifts, preferred_element_type=jnp.float32
    )
    grad_conv1 = first_output_gradient.astype(jnp.bfloat16)
    conv1_grad = kernel_grad(hidden_pad, grad_conv1)
    grad_hidden = conv_apply(framed(grad_conv1), conv1_w[::-1, ::-1], "HWOI") * image_window
    preactivation_gradient = grad_hidden * silu_slope(first_preactivation)
    start_term, norm1_grad = group_norm_backward(
        preactivation_gradient,
        first_normalized_input,
        first_inverse_deviation,
        first_norm_gain1,
        group_counts,
        image_window,
    )
    image_grad = (grad_middle + start_term) * image_window
    rows_sums = (
        lax.psum_scatter(norm1_grad, "rows", scatter_dimension=0, tiled=True),
        lax.psum_scatter(conv1_grad, "rows", scatter_dimension=3, tiled=True),
        lax.psum_scatter(second_norm_gradient2, "rows", scatter_dimension=0, tiled=True),
        lax.psum_scatter(conv2_grad, "rows", scatter_dimension=3, tiled=True),
        lax.psum_scatter(attn_gain_grad, "rows", scatter_dimension=0, tiled=True),
        lax.psum_scatter(qkv_grad, "rows", scatter_dimension=1, tiled=True),
        lax.psum_scatter(text_w_grad, "rows", scatter_dimension=0, tiled=True),
        lax.psum_scatter(proj_grad, "rows", scatter_dimension=1, tiled=True),
    )
    summed = (
        lax.psum(rows_sums[0].astype(jnp.bfloat16), "items").astype(jnp.float32),
        lax.psum(rows_sums[1].astype(jnp.bfloat16), "items").astype(jnp.float32),
        lax.psum(embed_w_grad.astype(jnp.bfloat16), "items").astype(jnp.float32),
        lax.psum(rows_sums[2].astype(jnp.bfloat16), "items").astype(jnp.float32),
        lax.psum(rows_sums[3].astype(jnp.bfloat16), "items").astype(jnp.float32),
        lax.psum(rows_sums[4].astype(jnp.bfloat16), "items").astype(jnp.float32),
        lax.psum(rows_sums[5].astype(jnp.bfloat16), "items").astype(jnp.float32),
        lax.psum(rows_sums[6].astype(jnp.bfloat16), "items").astype(jnp.float32),
        lax.psum(rows_sums[7].astype(jnp.bfloat16), "items").astype(jnp.float32),
    )
    return (
        output,
        image_grad,
        embed_grad,
        text_grad,
        summed[0],
        summed[1],
        summed[2],
        summed[3],
        summed[4],
        summed[5],
        summed[6],
        summed[7],
        summed[8],
    )


def solution(mesh):
    in_specs = (
        P("items", "rows", None, None),
        P("items", None),
        P("items", "rows", None),
        P("items", None),
        P(),
        P(),
        P(),
        P(),
        P(),
        P(),
        P(),
        P(),
        P(),
        P("items", "rows", None, None),
    )
    out_specs = (
        P("items", "rows", None, None),
        P("items", "rows", None, None),
        P("items", None),
        P("items", "rows", None),
        P("rows"),
        P(None, None, None, "rows"),
        P("rows", None),
        P("rows"),
        P(None, None, None, "rows"),
        P("rows"),
        P(None, "rows"),
        P("rows", None),
        P(None, "rows"),
    )
    return jax.shard_map(shards, mesh=mesh, in_specs=in_specs, out_specs=out_specs, check_vma=False)
```

profile of v0, /device:TPU:0, one launch (start us, length us, event | category | flops | bytes accessed | tf_op | source)
XLA Modules:
  0.0 1019.2 jit_solution(11134851617635650490)
XLA Ops:
  12.9 18.1 %all-reduce.11 = (f32[1,32]{1,0:T(1,128)S(1)}, f32[1,32]{1,0:T(1,128)S(1)}) all-reduce(f32[1,32]{1,0:T(1,128)S(1)} %bitcast.638, f32[1,32]{1,0:T(1,128)S(1)} %bitcast.634), channel_id=1, replica_groups=mesh['items'=4,'rows'=8] {'rows'}, use_global_device_ids=true, to_apply=%region_2.0 | all-reduce | flops 64 | bytes 512 | tf_op jit(solution)/shard_map/psum | solution.py:66
  48.3 4.9 convolution_select_fusion.3
  55.5 17.1 %all-reduce.10 = (f32[1,32]{1,0:T(1,128)S(1)}, f32[1,32]{1,0:T(1,128)S(1)}) all-reduce(f32[1,32]{1,0:T(1,128)S(1)} %bitcast.639, f32[1,32]{1,0:T(1,128)S(1)} %bitcast.635), channel_id=1, replica_groups=mesh['items'=4,'rows'=8] {'rows'}, use_global_device_ids=true, to_apply=%region_8.9 | all-reduce | flops 64 | bytes 512 | tf_op jit(solution)/shard_map/psum | solution.py:66
  89.4 4.9 convolution_select_fusion.2
  96.4 17.1 %all-reduce.9 = (f32[1,32]{1,0:T(1,128)S(1)}, f32[1,32]{1,0:T(1,128)S(1)}) all-reduce(f32[1,32]{1,0:T(1,128)S(1)} %bitcast.636, f32[1,32]{1,0:T(1,128)S(1)} %bitcast.640), channel_id=1, replica_groups=mesh['items'=4,'rows'=8] {'rows'}, use_global_device_ids=true, to_apply=%region_14.15 | all-reduce | flops 64 | bytes 512 | tf_op jit(solution)/shard_map/psum | solution.py:66
  126.5 45.0 %all-to-all-done = bf16[8,8,64,192]{3,2,1,0:T(8,128)(2,1)} async-done(((bf16[8,8,64,192]{3,2,1,0:T(8,128)(2,1)}), bf16[8,8,64,192]{3,2,1,0:T(8,128)(2,1)}, u32[]{:S(2)}, u32[]{:S(2)}) %all-to-all-start) | async-done | bytes 1572896 | tf_op jit(solution)/shard_map/all_to_all | solution.py:183
  176.2 64.5 %while.27 = (s32[]{:T(128)}, bf16[8,1,512,64]{2,3,1,0:T(8,128)(2,1)}, f32[8,1,512]{2,1,0:T(1,128)S(1)}, pred[1,4224]{1,0:T(4,128)(4,1)S(1)}, s32[8]{0:T(128)S(1)...) while((s32[]{:T(128)}, ...), condition=%wide.region_21.22_spmd, body=%wide.region_18.21_spmd.sunk | while | flops 570981888 | bytes 29426780 | solution.py:241
  249.4 4.4 all-to-all-start.2
  253.8 240.7 %while.28 = (s32[]{:T(128)}, f32[1,4224,64]{1,2,0:T(8,128)}, f32[1,4224,64]{1,2,0:T(8,128)S(1)}, bf16[8,1,512,64]{2,3,1,0:T(8,128)(2,1)}, pred[1,4224]{1,0:T(4,1...) while((s32[]{:T(128)}, f32[1,4224,64]{1,2,0:T(8,128)}, ...), condition=%wide.region_24.25_spmd.clone, body=%wide.region_22.24_spmd.clone.sunk | while | flops 1404968448 | bytes 134225152 | solution.py:299
  258.0 5.9 multiply_reduce_fusion.11
  263.9 9.1 multiply_convert_fusion.12
  287.8 5.9 multiply_reduce_fusion.11
  293.7 9.1 multiply_convert_fusion.12
  302.7 4.5 fusion.295
  317.9 5.9 multiply_reduce_fusion.11
  323.8 9.1 multiply_convert_fusion.12
  332.9 4.5 fusion.295
  348.0 5.9 multiply_reduce_fusion.11
  353.9 9.1 multiply_convert_fusion.12
  363.0 4.5 fusion.295
  378.2 5.9 multiply_reduce_fusion.11
  384.1 9.1 multiply_convert_fusion.12
  393.1 4.5 fusion.295
  408.3 5.9 multiply_reduce_fusion.11
  414.2 9.1 multiply_convert_fusion.12
  423.3 4.5 fusion.295
  438.4 5.9 multiply_reduce_fusion.11
  444.3 9.1 multiply_convert_fusion.12
  453.4 4.5 fusion.295
  468.6 5.9 multiply_reduce_fusion.11
  474.4 9.1 multiply_convert_fusion.12
  483.5 4.5 fusion.295
  505.7 5.2 copy.136
  510.9 5.2 all-to-all-start.4
  523.8 51.4 %all-to-all-done.4 = bf16[1,64,64,192]{3,2,0,1:T(8,128)(2,1)} async-done(((bf16[1,64,64,192]{3,2,0,1:T(8,128)(2,1)}), bf16[1,64,64,192]{3,2,0,1:T(8,128)(2,1)}, u32[]{:S(2)}, u32[]{:S(2)}) %all-to-all-start.4) | async-done | bytes 1572896 | tf_op jit(solution)/shard_map/all_to_all | solution.py:312
  589.8 8.2 all_to_all.27
  598.0 4.6 convolution_bitcast_fusion.1
  606.5 14.4 %all-reduce.8 = (f32[1,32]{1,0:T(1,128)S(1)}, f32[1,32]{1,0:T(1,128)S(1)}) all-reduce(f32[1,32]{1,0:T(1,128)S(1)} %bitcast.641, f32[1,32]{1,0:T(1,128)S(1)} %bitcast.633), channel_id=1, replica_groups=mesh['items'=4,'rows'=8] {'rows'}, use_global_device_ids=true, to_apply=%region_30.31 | all-reduce | flops 64 | bytes 512 | tf_op jit(solution)/shard_map/psum | solution.py:100
  636.3 9.6 copy.149
  655.4 5.0 convolution_select_fusion.1
  665.0 19.3 %all-reduce.7 = (f32[1,32]{1,0:T(1,128)S(1)}, f32[1,32]{1,0:T(1,128)S(1)}) all-reduce(f32[1,32]{1,0:T(1,128)S(1)} %bitcast.642, f32[1,32]{1,0:T(1,128)S(1)} %bitcast.637), channel_id=1, replica_groups=mesh['items'=4,'rows'=8] {'rows'}, use_global_device_ids=true, to_apply=%region_36.37 | all-reduce | flops 64 | bytes 512 | tf_op jit(solution)/shard_map/psum | solution.py:346
  701.2 9.6 copy.148
  719.8 5.1 convolution_select_fusion
  728.4 31.0 %all-reduce.6 = (f32[1,32]{1,0:T(1,128)S(1)}, f32[1,32]{1,0:T(1,128)S(1)}, bf16[1,512]{1,0:T(2,128)(2,1)S(1)}, bf16[1,512]{1,0:T(2,128)(2,1)S(1)}, bf16[512]{0:T...) all-reduce(f32[1,32]{1,0:T(1,128)S(1)} %bitcast.629, ...), channel_id=1, replica_groups=mesh['items'=4,'rows'=8] {'rows'}, use_global_device_ids=true, to_apply=%region_42.43 | all-reduce | flops 2624 | bytes 15872 | tf_op jit(solution)/shard_map/psum | solution.py:100
  765.7 56.3 %reduce-scatter.8.cloned.1.call-done = f32[3,3,512,64]{2,3,1,0:T(8,128)} async-done(((f32[3,3,512,512]{2,3,1,0:T(8,128)}), f32[3,3,512,64]{2,3,1,0:T(8,128)}) %reduce-scatter.8.cloned.1.call-update) | async-done | bytes 1179664 | tf_op jit(solution)/shard_map/reduce_scatter | solution.py:395
  824.2 97.9 %reduce-scatter.6.cloned.1.call-done = f32[3,3,512,64]{2,3,1,0:T(8,128)} async-done(((f32[3,3,512,512]{2,3,1,0:T(8,128)}), f32[3,3,512,64]{2,3,1,0:T(8,128)}) %reduce-scatter.6.cloned.1.call-update) | async-done | bytes 1179664 | tf_op jit(solution)/shard_map/reduce_scatter | solution.py:393
  932.4 10.3 %all-reduce.12 = (bf16[64]{0:T(256)(128)(2,1)S(1)}, bf16[64]{0:T(256)(128)(2,1)S(1)}, bf16[64]{0:T(256)(128)(2,1)S(1)}) all-reduce(bf16[64]{0:T(256)(128)(2,1)S(1)} %dynamic-slice.11, bf16[64]{0:T(256)(128)(2,1)S(1)} %dynamic-slice.10, bf16[64]{0:T(256)(128)(2,1)S(1)} %dynamic-slice.9), channel_id=1, replica_groups=mesh['items'=4,'rows'=8] {'items'}, use_global_device_ids=true, to_apply=%region_49.50 | all-reduce | flops 192 | bytes 768 | tf_op jit(solution)/shard_map/psum | solution.py:402
  951.8 51.0 %all-reduce.16.cloned.1.call-done = (bf16[256,1024]{0,1:T(8,128)(2,1)}, bf16[3,3,512,64]{2,3,1,0:T(8,128)(2,1)}, bf16[256,1024]{1,0:T(8,128)(2,1)}, bf16[3,3,512...) async-done(((bf16[256,1024]{0,1:T(8,128)(2,1)}, bf16[3,3,512,64]{2,3,1,0:T(8,128)(2,1)}, bf16[256,1024]{1,0:T(8,128)(2,1)}, ...) | async-done | bytes 2490384 | tf_op jit(solution)/shard_map/psum | solution.py:409
  (589 shorter events, 343.5 us)
Async XLA Ops:
  7.2 69.3 %copy-start = (bf16[512,512]{1,0:T(8,128)(2,1)S(1)}, bf16[512,512]{1,0:T(8,128)(2,1)}, u32[]{:S(2)}) copy-start(bf16[512,512]{1,0:T(8,128)(2,1)} %param.30) | copy-start | bytes 1572868
  7.2 36.2 %copy-start.32 = (bf16[1,2048]{1,0:T(2,128)(2,1)S(1)}, bf16[1,2048]{1,0:T(2,128)(2,1)}, u32[]{:S(2)}) copy-start(bf16[1,2048]{1,0:T(2,128)(2,1)} %param.19) | copy-start | bytes 12292
  11.2 102.7 %copy-start.25 = (f32[8,64]{1,0:T(8,128)}, f32[8,64]{1,0:T(8,128)S(1)}, u32[]{:S(2)}) copy-start(f32[8,64]{1,0:T(8,128)S(1)} %and_convert_fusion) | copy-start | bytes 6148
  33.9 12.4 %copy-start.17 = (bf16[1,8,64,512]{3,2,1,0:T(8,128)(2,1)}, bf16[1,8,64,512]{3,2,1,0:T(8,128)(2,1)S(1)}, u32[]{:S(2)}) copy-start(bf16[1,8,64,512]{3,2,1,0:T(8,128)(2,1)S(1)} %multiply_convert_fusion.6) | copy-start | bytes 1572868
  33.9 12.3 %collective-permute-start = (bf16[1,1,64,512]{3,2,1,0:T(8,128)(2,1)S(1)}, bf16[1,1,64,512]{3,2,1,0:T(8,128)(2,1)S(1)}, u32[]{:S(2)}, u32[]{:S(2)}) collective-permute-start(bf16[1,1,64,512]{3,2,1,0:T(8,128)(2,1)S(1)} %get-tuple-element.345), channel_id=1, source_target_pairs={{0,1},{1,2},{2,3},{3,4},{4,5},{5,6},{6,7},{8,9},{9,10},{10,11},{11... | collective-permute-start | bytes 196616 | tf_op jit(solution)/shard_map/ppermute | solution.py:21
  35.2 11.1 %collective-permute-start.1 = (bf16[1,1,64,512]{3,2,1,0:T(8,128)(2,1)S(1)}, bf16[1,1,64,512]{3,2,1,0:T(8,128)(2,1)S(1)}, u32[]{:S(2)}, u32[]{:S(2)}) collective-permute-start(bf16[1,1,64,512]{3,2,1,0:T(8,128)(2,1)S(1)} %get-tuple-element.346), channel_id=1, source_target_pairs={{1,0},{2,1},{3,2},{4,3},{5,4},{6,5},{7,6},{9,8},{10,9},{11,10},{12... | collective-permute-start | bytes 196616 | tf_op jit(solution)/shard_map/ppermute | solution.py:22
  40.0 45.7 %all-to-all-start.1 = ((bf16[8,16,128]{2,1,0:T(8,128)(2,1)}), bf16[8,16,128]{2,1,0:T(8,128)(2,1)S(1)}, u32[]{:S(2)}, u32[]{:S(2)}) async-start(bf16[8,16,128]{2,1,0:T(8,128)(2,1)} %fusion.72), calls=%async_computation.1 | async-start | bytes 65536 | tf_op jit(solution)/shard_map/all_to_all | solution.py:190
  46.2 26.8 %copy-start.55 = (f32[1,512]{1,0:T(1,128)}, f32[1,512]{1,0:T(1,128)S(1)}, u32[]{:S(2)}) copy-start(f32[1,512]{1,0:T(1,128)S(1)} %get-tuple-element.349) | copy-start | bytes 6148
  46.2 26.7 %copy-start.62 = (f32[1,512]{1,0:T(1,128)}, f32[1,512]{1,0:T(1,128)S(1)}, u32[]{:S(2)}) copy-start(f32[1,512]{1,0:T(1,128)S(1)} %get-tuple-element.350) | copy-start | bytes 6148
  53.2 19.8 %copy-start.60 = (f32[512]{0:T(512)S(1)}, f32[512]{0:T(512)}, u32[]{:S(2)}) copy-start(f32[512]{0:T(512)} %param.25) | copy-start | bytes 6148
  53.2 23.3 %copy-start.12 = (bf16[1,8,64,512]{3,2,1,0:T(8,128)(2,1)S(1)}, bf16[1,8,64,512]{3,2,1,0:T(8,128)(2,1)}, u32[]{:S(2)}) copy-start(bf16[1,8,64,512]{3,2,1,0:T(8,128)(2,1)} %param.31) | copy-start | bytes 1572868
  54.0 26.9 %copy-start.4 = (f32[8,1,64,512]{3,0,2,1:T(8,128)}, f32[8,1,64,512]{3,0,2,1:T(8,128)S(1)}, u32[]{:S(2)}) copy-start(f32[8,1,64,512]{3,0,2,1:T(8,128)S(1)} %slice.185) | copy-start | bytes 3145732
  73.9 9.8 copy-start.19
  73.9 9.8 collective-permute-start.2
  75.2 8.5 collective-permute-start.3
  85.7 32.4 %all-to-all-start.3 = ((bf16[8,2,16384]{2,1,0:T(2,128)(2,1)}), bf16[8,2,16384]{2,1,0:T(2,128)(2,1)S(1)}, u32[]{:S(2)}, u32[]{:S(2)}) async-start(bf16[8,2,16384]{2,1,0:T(2,128)(2,1)} %reshape.955), calls=%async_computation.3 | async-start | bytes 1048576 | tf_op jit(solution)/shard_map/all_to_all | solution.py:258
  94.3 19.6 %copy-start.58 = (f32[512]{0:T(512)S(1)}, f32[512]{0:T(512)}, u32[]{:S(2)}) copy-start(f32[512]{0:T(512)} %param.27) | copy-start | bytes 6148
  96.0 22.1 %copy-start.6 = (f32[1,8,64,512]{3,2,1,0:T(8,128)}, f32[1,8,64,512]{3,2,1,0:T(8,128)S(1)}, u32[]{:S(2)}) copy-start(f32[1,8,64,512]{3,2,1,0:T(8,128)S(1)} %get-tuple-element.323) | copy-start | bytes 3145732
  118.1 53.4 %all-to-all-start = ((bf16[8,8,64,192]{3,2,1,0:T(8,128)(2,1)}), bf16[8,8,64,192]{3,2,1,0:T(8,128)(2,1)}, u32[]{:S(2)}, u32[]{:S(2)}) async-start(bf16[8,8,64,192]{3,2,1,0:T(8,128)(2,1)} %copy.123), calls=%async_computation | async-start | bytes 4194304 | tf_op jit(solution)/shard_map/all_to_all | solution.py:183
  249.4 261.5 %all-to-all-start.2 = ((bf16[8,2,16384]{2,1,0:T(2,128)(2,1)}), bf16[8,2,16384]{2,1,0:T(2,128)(2,1)}, u32[]{:S(2)}, u32[]{:S(2)}) async-start(bf16[8,2,16384]{2,1,0:T(2,128)(2,1)} %reshape.959), calls=%async_computation.2 | async-start | bytes 1048576 | tf_op jit(solution)/shard_map/all_to_all | solution.py:244
  363.0 8.9 slice-start
  363.0 8.9 slice-start.1
  510.9 10.1 copy-start.13
  510.9 10.1 copy-start.26
  510.9 64.2 %all-to-all-start.4 = ((bf16[1,64,64,192]{3,2,0,1:T(8,128)(2,1)}), bf16[1,64,64,192]{3,2,0,1:T(8,128)(2,1)}, u32[]{:S(2)}, u32[]{:S(2)}) async-start(bf16[1,64,64,192]{3,2,0,1:T(8,128)(2,1)} %copy.136), calls=%async_computation.4 | async-start | bytes 4194304 | tf_op jit(solution)/shard_map/all_to_all | solution.py:312
  516.2 244.2 %reduce-scatter.14.cloned.1.call-start = ((), (), s32[]{:S(2)}) async-start(), calls=%async_computation.15 | async-start | bytes 1179648 | tf_op jit(solution)/shard_map/reduce_scatter | solution.py:399
  518.9 60.4 %copy-start.11 = (bf16[64,1,64,64]{3,2,1,0:T(8,128)(2,1)}, bf16[64,1,64,64]{3,2,1,0:T(8,128)(2,1)S(1)}, u32[]{:S(2)}) copy-start(bf16[64,1,64,64]{3,2,1,0:T(8,128)(2,1)S(1)} %reshape.960) | copy-start | bytes 1572868
  523.7 59.9 %copy-start.7 = (f32[1,8,64,512]{3,2,1,0:T(8,128)S(1)}, f32[1,8,64,512]{3,2,1,0:T(8,128)}, u32[]{:S(2)}) copy-start(f32[1,8,64,512]{3,2,1,0:T(8,128)} %copy-done.6) | copy-start | bytes 3145732
  523.7 59.9 %copy-start.48 = (f32[512]{0:T(512)S(1)}, f32[512]{0:T(512)}, u32[]{:S(2)}) copy-start(f32[512]{0:T(512)} %copy-done.47) | copy-start | bytes 6148
  523.7 59.9 %copy-start.50 = (f32[512]{0:T(512)S(1)}, f32[512]{0:T(512)}, u32[]{:S(2)}) copy-start(f32[512]{0:T(512)} %copy-done.49) | copy-start | bytes 6148
  523.7 59.9 %copy-start.59 = (f32[512]{0:T(512)S(1)}, f32[512]{0:T(512)}, u32[]{:S(2)}) copy-start(f32[512]{0:T(512)} %param.27) | copy-start | bytes 6148
  523.8 238.2 %reduce-scatter.10.cloned.1.call-start = ((), (), s32[]{:S(2)}) async-start(), calls=%async_computation.13 | async-start | bytes 3538944 | tf_op jit(solution)/shard_map/reduce_scatter | solution.py:397
  583.7 14.3 %copy-start.30 = (bf16[1,16,2048]{2,1,0:T(8,128)(2,1)S(1)}, bf16[1,16,2048]{2,1,0:T(8,128)(2,1)}, u32[]{:S(2)}) copy-start(bf16[1,16,2048]{2,1,0:T(8,128)(2,1)} %param.20) | copy-start | bytes 196612
  587.9 175.8 %reduce-scatter.12.cloned.1.call-start = ((), (), s32[]{:S(2)}) async-start(), calls=%async_computation.14 | async-start | bytes 9437184 | tf_op jit(solution)/shard_map/reduce_scatter | solution.py:398
  602.6 219.5 %reduce-scatter.8.cloned.1.call-start = ((), (), s32[]{:S(2)}) async-start(), calls=%async_computation.12 | async-start | bytes 10616832 | tf_op jit(solution)/shard_map/reduce_scatter | solution.py:395
  605.8 18.7 %copy-start.10 = (f32[8,64,512]{2,1,0:T(8,128)}, f32[8,64,512]{2,1,0:T(8,128)S(1)}, u32[]{:S(2)}) copy-start(f32[8,64,512]{2,1,0:T(8,128)S(1)} %get-tuple-element.358) | copy-start | bytes 3145732
  605.8 18.7 %copy-start.41 = (bf16[1,1,64,512]{3,2,1,0:T(8,128)(2,1)S(1)}, bf16[1,1,64,512]{3,2,1,0:T(8,128)(2,1)}, u32[]{:S(2)}) copy-start(bf16[1,1,64,512]{3,2,1,0:T(8,128)(2,1)} %copy-done.40) | copy-start | bytes 196612
  621.8 13.0 %copy-start.21 = (bf16[1,8,64,512]{3,2,1,0:T(8,128)(2,1)}, bf16[1,8,64,512]{3,2,1,0:T(8,128)(2,1)S(1)}, u32[]{:S(2)}) copy-start(bf16[1,8,64,512]{3,2,1,0:T(8,128)(2,1)S(1)} %multiply_convert_fusion.3) | copy-start | bytes 1572868
  645.9 9.4 copy-start.67
  645.9 276.2 %reduce-scatter.6.cloned.1.call-start = ((), (), s32[]{:S(2)}) async-start(), calls=%async_computation.11 | async-start | bytes 10616832 | tf_op jit(solution)/shard_map/reduce_scatter | solution.py:393
  647.0 3.0 collective-permute-start.4
  648.7 3.1 collective-permute-start.5
  661.6 27.8 %copy-start.37 = (bf16[1,1,64,512]{3,2,1,0:T(8,128)(2,1)S(1)}, bf16[1,1,64,512]{3,2,1,0:T(8,128)(2,1)}, u32[]{:S(2)}) copy-start(bf16[1,1,64,512]{3,2,1,0:T(8,128)(2,1)} %copy-done.36) | copy-start | bytes 196612
  686.7 13.0 %copy-start.15 = (bf16[1,8,64,512]{3,2,1,0:T(8,128)(2,1)}, bf16[1,8,64,512]{3,2,1,0:T(8,128)(2,1)S(1)}, u32[]{:S(2)}) copy-start(bf16[1,8,64,512]{3,2,1,0:T(8,128)(2,1)S(1)} %multiply_convert_fusion.2) | copy-start | bytes 1572868
  710.8 292.0 %all-reduce.16.cloned.1.call-start = ((), (), s32[]{:S(2)}) async-start(), calls=%async_computation.16 | async-start | bytes 4980736 | tf_op jit(solution)/shard_map/psum | solution.py:409
  711.8 2.6 collective-permute-start.6
  713.1 3.1 collective-permute-start.7
  760.4 163.9 %copy-start.65 = (u32[32]{0:T(128)S(1)}, u32[32]{0:T(128)}, u32[]{:S(2)}) copy-start(u32[32]{0:T(128)} %constant.136) | copy-start | bytes 388
  (86 other events, 351.4 us)
Sparse Core Ops, SparseCore 0:
  523.8 38.5 reduce-scatter.13
  588.0 40.0 reduce-scatter.9
  630.4 90.1 reduce-scatter.11
  722.8 99.2 reduce-scatter.7
  824.2 97.8 reduce-scatter.5
  926.9 75.7 all-reduce.15
where the time goes:
time: 1030 us; the launch traced here: 1020 us
  waiting for transfers between devices  305 us (30%)
  matrix products  285 us (28%)
  blocking collectives  135 us (13%)
  other arithmetic  134 us (13%)
  local copies, waits for them, and re-layouts  98.1 us (10%)
  starting transfers between devices  32.4 us (3%)
  between operations  17.7 us (2%)
  loops' own time  11.3 us (1%)
    reduce_scatter x1, waiting for transfers between devices, shards(): lax.psum_scatter(conv1_grad, 'rows', scatter_dimension=3, tiled=True)  97.9 us
    convert_element_type x8, other arithmetic, backward_block(): grad_scores = (attn_probs * (grad_probs - jnp.sum(grad_probs * attn_probs...  72.6 us
    reduce_scatter x1, waiting for transfers between devices, shards(): lax.psum_scatter(conv2_grad, 'rows', scatter_dimension=3, tiled=True)  56.3 us
    psum x3, blocking collectives, group_norm_forward(): lax.psum((jnp.sum(shaped, axis=(1, 2, 4)), jnp.sum(shaped * shaped, axis=...  52.3 us
    all_to_all x1, waiting for transfers between devices, shards(): lax.all_to_all(image_qkv_grad, 'rows', split_axis=1, concat_axis=0, tiled...  51.4 us
    psum x1, waiting for transfers between devices, shards(): lax.psum(rows_sums[6].astype(jnp.bfloat16), 'items').astype(jnp.float32)  51 us
    dot_general x8, matrix products, backward_block(): jnp.einsum('pqd,pkd->pqk', grad_block, values, preferred_element_type=jnp...  47 us
    psum x2, blocking collectives, group_norm_backward(): lax.psum((jnp.sum(shaped_grad, axis=(1, 2, 4)), jnp.sum(shaped_grad * res...  45.5 us
  transfers between devices with their start and end apart: 19, of which 7 were waited for; matrix products, arithmetic and copies ran while one was open for 41% of the time, Pallas kernels for 0%

commit v1 on v0

--- a/solution.py
+++ b/solution.py
@@ -1,14 +1,186 @@
+import functools
+
 import jax
 import jax.numpy as jnp
 from jax import lax
+from jax.experimental import pallas as pl
+from jax.experimental.pallas import tpu as pltpu
 from jax.sharding import PartitionSpec as P
 
 GROUPS = 32
 HEADS = 8
+F32, BF16 = jnp.float32, jnp.bfloat16
+NEG = -1e30
+
+
+def dot(a, b, ca, cb):
+    return lax.dot_general(a, b, (((ca,), (cb,)), ((), ())), preferred_element_type=F32)
+
+def attention_kernel(width, step, bq, ext_ref, qkv_ref, text_ref, go_ref, out_ref, dqkv_ref, dtext_ref,
+                     kn, vn, kt, vt, s0, s1, e0, e1, dkt, dvt):
+    scores, raised = (s0, s1), (e0, e1)
+    chunks, _, span = qkv_ref.shape
+    tlen = text_ref.shape[0]
+    d = go_ref.shape[1]
+    pix = chunks * span
+    keys = pix + tlen
+    steps = keys // step
+    rows_ok, cols_ok = ext_ref[0, 0], ext_ref[0, 1]
+    def stage(c, carry):
+        base = pl.multiple_of(c * span, span)
+        pos = base + lax.broadcasted_iota(jnp.int32, (16, span), 1)
+        row = lax.broadcasted_iota(jnp.int32, (16, span), 0)
+        ok = (pos // width < rows_ok) & (pos % width < cols_ok)
+        extra = jnp.where((row == 0) & jnp.logical_not(ok), NEG, 0.0)
+        k = qkv_ref[c, d:2 * d, :]
+        v = qkv_ref[c, 2 * d:, :]
+        kt[:, pl.ds(base, span)] = k
+        vt[:, pl.ds(base, span)] = v
+        rest = jnp.zeros((128 - d - 16, span), F32)
+        ka = jnp.concatenate([k.astype(F32), extra, rest], axis=0)
+        va = jnp.concatenate([v.astype(F32), jnp.where(row < 3, 1.0, 0.0), rest], axis=0)
+        kn[pl.ds(base, span), :] = ka.T.astype(BF16)
+        vn[pl.ds(base, span), :] = va.T.astype(BF16)
+        return carry
+    lax.fori_loop(0, chunks, stage, 0)
+    tk = text_ref[:, :d].astype(F32)
+    tv = text_ref[:, d:].astype(F32)
+    kt[:, pix:] = tk.T.astype(BF16)
+    vt[:, pix:] = tv.T.astype(BF16)
+    lanes = lax.broadcasted_iota(jnp.int32, (tlen, 128 - d), 1)
+    kn[pix:, :] = jnp.concatenate([tk, jnp.zeros((tlen, 128 - d), F32)], axis=1).astype(BF16)
+    vn[pix:, :] = jnp.concatenate([tv, jnp.where(lanes < 3, 1.0, 0.0)], axis=1).astype(BF16)
+    dkt[...] = jnp.zeros_like(dkt)
+    dvt[...] = jnp.zeros_like(dvt)
+
+    low_peak = jnp.full((8, bq), -3e38, F32)
+
+    def q_aug(c, half):
+        q = qkv_ref[c, :d, half * bq:(half + 1) * bq].astype(F32) * (d ** -0.5)
+        r = lax.broadcasted_iota(jnp.int32, (128 - d, bq), 0)
+        return jnp.concatenate([q, jnp.where(r == 0, 1.0, 0.0)], axis=0).astype(BF16)
+
+    def run(score, exp, back):
+        def body(j, carry):
+            pk, total, acc, dq = carry
+            at = pl.ds(pl.multiple_of(j * step, step), step)
+            if score:
+                slot, qa = score
+                s = dot(kn[at, :], qa, 1, 0)
+                scores[slot][at, :] = s
+                pk = jnp.maximum(pk, jnp.max(s.reshape(step // 8, 8, bq), axis=0))
+            if exp:
+                slot, peak = exp
+                e = jnp.exp(scores[slot][at, :] - peak)
+                total = total + jnp.sum(e.reshape(step // 8, 8, bq), axis=0)
+                low = e.astype(BF16)
+                raised[slot][at, :] = low
+                acc = acc + dot(vt[:, at], low, 1, 0)
+            if back:
+                slot, goa, gs, q = back
+                dp = dot(vn[at, :], goa, 1, 0)
+                e = raised[slot][at, :]
+                ds = (e.astype(F32) * dp).astype(BF16)
+                dvt[:, at] += dot(gs, e, 1, 1)
+                dkt[:, at] += dot(q, ds, 1, 1)
+                dq = dq + dot(kt[:, at], ds, 1, 0)
+            return pk, total, acc, dq
+        init = (low_peak, jnp.zeros((8, bq), F32), jnp.zeros((d, bq), F32), jnp.zeros((d, bq), F32))
+        return lax.fori_loop(0, steps, body, init)
+
+    def finish_exp(c, half, total, acc):
+        inv = 1.0 / jnp.sum(total, axis=0, keepdims=True)
+        o = acc * inv
+        cols = slice(half * bq, (half + 1) * bq)
+        out_ref[c, :, cols] = o.astype(BF16)
+        go = go_ref[c, :, cols].astype(F32)
+        nd = -jnp.sum(go * o, axis=0, keepdims=True) * inv
+        gs = go * inv
+        hi = nd.astype(BF16).astype(F32)
+        mid = (nd - hi).astype(BF16).astype(F32)
+        lo = nd - hi - mid
+        r = lax.broadcasted_iota(jnp.int32, (16, bq), 0)
+        extra = jnp.where(r == 0, hi, jnp.where(r == 1, mid, jnp.where(r == 2, lo, 0.0)))
+        goa = jnp.concatenate([gs, extra, jnp.zeros((128 - d - 16, bq), F32)], axis=0).astype(BF16)
+        return goa
+
+    def put_dq(c, half, dq):
+        dqkv_ref[c, :d, half * bq:(half + 1) * bq] = (dq * (d ** -0.5)).astype(BF16)
+
+    def top(pk):
+        return jnp.max(pk, axis=0, keepdims=True)
+
+    def q_of(c, half):
+        return qkv_ref[c, :d, half * bq:(half + 1) * bq]
+
+    pk, _, _, _ = run((0, q_aug(0, 0)), None, None)
+    pk, total, acc, _ = run((1, q_aug(0, 1)), (0, top(pk)), None)
+    goa = finish_exp(0, 0, total, acc)
+
+    def two(h, carry):
+        pk, goa = carry
+        pk2, total, acc, dq = run((0, q_aug(h + 1, 0)), (1, top(pk)), (0, goa, goa[:d], q_of(h, 0)))
+        put_dq(h, 0, dq)
+        goa = finish_exp(h, 1, total, acc)
+        pk3, total, acc, dq = run((1, q_aug(h + 1, 1)), (0, top(pk2)), (1, goa, goa[:d], q_of(h, 1)))
+        put_dq(h, 1, dq)
+        return pk3, finish_exp(h + 1, 0, total, acc)
+    pk, goa = lax.fori_loop(0, chunks - 1, two, (pk, goa))
+    last = chunks - 1
+    _, total, acc, dq = run(None, (1, top(pk)), (0, goa, goa[:d], q_of(last, 0)))
+    put_dq(last, 0, dq)
+    goa = finish_exp(last, 1, total, acc)
+    _, _, _, dq = run(None, None, (1, goa, goa[:d], q_of(last, 1)))
+    put_dq(last, 1, dq)
+
+    def finish(c, carry):
+        at = pl.ds(pl.multiple_of(c * span, span), span)
+        dqkv_ref[c, d:2 * d, :] = (dkt[:, at] * (d ** -0.5)).astype(BF16)
+        dqkv_ref[c, 2 * d:, :] = dvt[:, at].astype(BF16)
+        return carry
+    lax.fori_loop(0, chunks, finish, 0)
+    dtext_ref[:d, :] = (dkt[:, pix:] * (d ** -0.5)).astype(BF16)
+    dtext_ref[d:, :] = dvt[:, pix:].astype(BF16)
+
+def attention(ext, qkv, text, go, width):
+    chunks, wide, span = qkv.shape
+    d = wide // 3
+    tlen = text.shape[0]
+    keys = chunks * span + tlen
+    bq = span // 2
+    lanes = keys // 128
+    step = 128 * max(n for n in range(1, 12) if lanes % n == 0)
+    vm = pl.BlockSpec(memory_space=pltpu.VMEM)
+    flops = 2 * 6 * chunks * span * keys * d
+    return pl.pallas_call(
+        functools.partial(attention_kernel, width, step, bq),
+        out_shape=(
+            jax.ShapeDtypeStruct(go.shape, BF16),
+            jax.ShapeDtypeStruct(qkv.shape, BF16),
+            jax.ShapeDtypeStruct((2 * d, tlen), BF16),
+        ),
+        in_specs=[pl.BlockSpec(memory_space=pltpu.SMEM), vm, vm, vm],
+        out_specs=(vm, vm, vm),
+        scratch_shapes=[
+            pltpu.VMEM((keys, 128), BF16),
+            pltpu.VMEM((keys, 128), BF16),
+            pltpu.VMEM((d, keys), BF16),
+            pltpu.VMEM((d, keys), BF16),
+            pltpu.VMEM((keys, bq), F32),
+            pltpu.VMEM((keys, bq), F32),
+            pltpu.VMEM((keys, bq), BF16),
+            pltpu.VMEM((keys, bq), BF16),
+            pltpu.VMEM((d, keys), F32),
+            pltpu.VMEM((d, keys), F32),
+        ],
+        compiler_params=pltpu.CompilerParams(vmem_limit_bytes=56 << 20),
+        cost_estimate=pl.CostEstimate(
+            flops=4 * flops, bytes_accessed=16 * chunks * span * d, transcendentals=chunks * span * keys
+        ),
+    )(ext, qkv, text, go)
 
 
 eps = 1e-05
-negative = -1e30
 
 
 def padded_2(shard, sides, width):
@@ -47,9 +219,11 @@
         for tap_col in range(3):
             shifted = padded[:, tap_row : tap_row + rows_dev, tap_col : tap_col + width]
             taps.append(
-                jnp.einsum("irwc,irwk->ck", shifted, grad_out, preferred_element_type=jnp.float32)
+                jnp.einsum(
+                    "irwk,irwc->kc", grad_out, shifted, preferred_element_type=jnp.float32
+                ).astype(BF16)
             )
-    return jnp.stack(taps).reshape(3, 3, padded.shape[3], grad_out.shape[3])
+    return jnp.stack(taps, axis=1)
 
 
 def silu_slope(values):
@@ -173,159 +347,87 @@
     qkv_shaped = qkv_w.reshape(channels, HEADS, 3 * head_dim)
     text_shaped = text_w.reshape(text_w.shape[0], HEADS, 2 * head_dim)
     proj_shaped = proj_w.reshape(HEADS, head_dim, channels)
+    pixels = rows_dev * width
+    group = max(1, 512 // pixels)
+    span = group * pixels
+    chunks = parts // group
+
+    def to_pairs(values):
+        wide = values.shape[1]
+        moved = lax.all_to_all(values, "rows", split_axis=0, concat_axis=0, tiled=True)
+        moved = moved.reshape(chunks, group, pairs, wide, pixels)
+        return jnp.transpose(moved, (2, 0, 3, 1, 4)).reshape(pairs, chunks, wide, span)
+
+    def from_pairs(values):
+        wide = values.shape[2]
+        moved = values.reshape(pairs, chunks, wide, group, pixels)
+        moved = jnp.transpose(moved, (1, 3, 0, 2, 4)).reshape(parts * pairs, wide, pixels)
+        return lax.all_to_all(moved, "rows", split_axis=0, concat_axis=0, tiled=True)
+
+    attn_flat = attention_input.reshape(images, pixels, channels)
     qkv_pix = jnp.einsum(
-        "irwc,chk->ihrwk", attention_input, qkv_shaped, preferred_element_type=jnp.float32
-    ).astype(jnp.bfloat16)
+        "ipc,chk->ihkp", attn_flat, qkv_shaped, preferred_element_type=jnp.float32
+    ).astype(BF16)
     text_pix = jnp.einsum(
         "itc,chk->ihtk", text, text_shaped, preferred_element_type=jnp.float32
-    ).astype(jnp.bfloat16)
-    qkv_pair, text_pair = (
-        lax.all_to_all(
-            qkv_pix.reshape((images * HEADS,) + qkv_pix.shape[2:]),
-            "rows",
-            split_axis=0,
-            concat_axis=1,
-            tiled=True,
-        ),
-        lax.all_to_all(
-            text_pix.reshape((images * HEADS,) + text_pix.shape[2:]),
-            "rows",
-            split_axis=0,
-            concat_axis=1,
-            tiled=True,
-        ),
-    )
-    frame_rows = qkv_pair.shape[1]
-    text_len = text_pair.shape[1]
-    tokens = frame_rows * width
+    ).astype(BF16)
+    grad_out = cotangent.astype(jnp.float32)
+    grad_proj = (grad_out * image_window).astype(BF16).reshape(images, pixels, channels)
+    grad_heads = jnp.einsum(
+        "ipc,hdc->ihdp", grad_proj, proj_shaped, preferred_element_type=jnp.float32
+    ).astype(BF16)
+    grad_pair = to_pairs(grad_heads.reshape(images * HEADS, head_dim, pixels))
+    text_pair = lax.all_to_all(
+        text_pix.reshape(images * HEADS, text.shape[1], 2 * head_dim),
+        "rows",
+        split_axis=0,
+        concat_axis=0,
+        tiled=True,
+    )
+    text_pair = jnp.moveaxis(
+        text_pair.reshape(parts, pairs, text.shape[1], 2 * head_dim), 1, 0
+    ).reshape(pairs, parts * text.shape[1], 2 * head_dim)
+    text_share = text.shape[2] // parts
+    text_cols = lax.all_to_all(text, "rows", split_axis=2, concat_axis=1, tiled=True)
+    text_cols = lax.all_gather(text_cols, "items", axis=0, tiled=True)
+    qkv_pair = to_pairs(qkv_pix.reshape(images * HEADS, 3 * head_dim, pixels))
     pair_index = lax.axis_index("rows") * pairs + jnp.arange(pairs, dtype=jnp.int32)
     pick = ((pair_index // HEADS)[:, None] == jnp.arange(images, dtype=jnp.int32)[None, :]).astype(
         jnp.int32
     )
     pair_extent = jnp.sum(pick[:, :, None] * extent[None, :, :], axis=1)
-    pixel_ok = (
-        jnp.arange(frame_rows, dtype=jnp.int32)[None, :, None] < pair_extent[:, 0, None, None]
-    ) & (colpos[None, None, :] < pair_extent[:, 1, None, None])
-    keys_ok = jnp.concatenate(
-        [jnp.ones((pairs, text_len), jnp.bool_), pixel_ok.reshape(pairs, tokens)], axis=1
-    )
-    flat = qkv_pair.reshape(pairs, tokens, 3 * head_dim)
-    queries = flat[:, :, :head_dim]
-    keys = jnp.concatenate(
-        [text_pair[:, :, :head_dim], flat[:, :, head_dim : 2 * head_dim]], axis=1
-    )
-    values = jnp.concatenate([text_pair[:, :, head_dim:], flat[:, :, 2 * head_dim :]], axis=1)
-    block = min(512, tokens)
-    blocks = tokens // block
-    factor = head_dim ** (-0.5)
-
-    def scores_of(index):
-        query_block = lax.dynamic_slice_in_dim(queries, index * block, block, 1)
-        scores = (
-            jnp.einsum("pqd,pkd->pqk", query_block, keys, preferred_element_type=jnp.float32)
-            * factor
-        )
-        return (query_block, jnp.where(keys_ok[:, None, :], scores, negative))
-
-    def forward_block(index):
-        query_block, scores = scores_of(index)
-        peak = jnp.max(scores, axis=2, keepdims=True)
-        raised = jnp.exp(scores - peak)
-        total = jnp.sum(raised, axis=2, keepdims=True)
-        attn_probs = (raised / total).astype(jnp.bfloat16)
-        attended = jnp.einsum(
-            "pqk,pkd->pqd", attn_probs, values, preferred_element_type=jnp.float32
-        )
-        return (attended.astype(jnp.bfloat16), (peak + jnp.log(total))[:, :, 0])
-
-    attended, logsum = lax.map(forward_block, jnp.arange(blocks))
-    attended = jnp.moveaxis(attended, 0, 1).reshape(pairs, frame_rows, width, head_dim)
-    logsum = jnp.moveaxis(logsum, 0, 1).reshape(pairs, tokens)
-    heads_out = lax.all_to_all(attended, "rows", split_axis=1, concat_axis=0, tiled=True)
-    heads_out = heads_out.reshape(images, HEADS, rows_dev, width, head_dim)
+    results = [
+        attention(pair_extent[p : p + 1], qkv_pair[p], text_pair[p], grad_pair[p], width)
+        for p in range(pairs)
+    ]
+    attended, qkv_grad_pair, text_grad_pair = (jnp.stack(parts_of) for parts_of in zip(*results))
+    qkv_back = from_pairs(qkv_grad_pair).reshape(images, HEADS, 3 * head_dim, pixels)
+    heads_out = from_pairs(attended).reshape(images, HEADS, head_dim, pixels)
+    text_back = lax.all_gather(text_grad_pair, "rows", axis=0, tiled=True)
+    text_back = text_back.reshape(images, HEADS, 2 * head_dim, parts * text.shape[1])
+    text_all = lax.all_gather(text_back, "items", axis=0, tiled=True)
+    own_text = lax.dynamic_slice_in_dim(
+        text_back, lax.axis_index("rows") * text.shape[1], text.shape[1], 3
+    )
     projected = jnp.einsum(
-        "ihrwd,hdc->irwc", heads_out, proj_shaped, preferred_element_type=jnp.float32
-    )
-    output = (middle_output + projected * image_window).astype(jnp.bfloat16)
-    grad_out = cotangent.astype(jnp.float32)
-    grad_proj = (grad_out * image_window).astype(jnp.bfloat16)
+        "ihdp,hdc->ipc", heads_out, proj_shaped, preferred_element_type=jnp.float32
+    ).reshape(image.shape)
+    output = (middle_output + projected * image_window).astype(BF16)
     proj_grad = jnp.einsum(
-        "ihrwd,irwc->hdc", heads_out, grad_proj, preferred_element_type=jnp.float32
+        "ipc,ihdp->chd", grad_proj, heads_out, preferred_element_type=jnp.float32
     ).reshape(channels, channels)
-    grad_heads = jnp.einsum(
-        "irwc,hdc->ihrwd", grad_proj, proj_shaped, preferred_element_type=jnp.float32
-    ).astype(jnp.bfloat16)
-    grad_pair = lax.all_to_all(
-        grad_heads.reshape((images * HEADS,) + grad_heads.shape[2:]),
-        "rows",
-        split_axis=0,
-        concat_axis=1,
-        tiled=True,
-    )
-    grad_flat = grad_pair.reshape(pairs, tokens, head_dim)
-
-    def backward_block(carry, index):
-        key_grad, value_grad = carry
-        query_block, scores = scores_of(index)
-        lse_block = lax.dynamic_slice_in_dim(logsum, index * block, block, 1)
-        attn_probs = jnp.exp(scores - lse_block[:, :, None])
-        grad_block = lax.dynamic_slice_in_dim(grad_flat, index * block, block, 1)
-        grad_probs = jnp.einsum(
-            "pqd,pkd->pqk", grad_block, values, preferred_element_type=jnp.float32
-        )
-        grad_scores = (
-            attn_probs * (grad_probs - jnp.sum(grad_probs * attn_probs, axis=2, keepdims=True))
-        ).astype(jnp.bfloat16)
-        query_grad = (
-            jnp.einsum("pqk,pkd->pqd", grad_scores, keys, preferred_element_type=jnp.float32)
-            * factor
-        )
-        key_grad = (
-            key_grad
-            + jnp.einsum(
-                "pqk,pqd->pkd", grad_scores, query_block, preferred_element_type=jnp.float32
-            )
-            * factor
-        )
-        value_grad = value_grad + jnp.einsum(
-            "pqk,pqd->pkd",
-            attn_probs.astype(jnp.bfloat16),
-            grad_block,
-            preferred_element_type=jnp.float32,
-        )
-        return ((key_grad, value_grad), query_grad)
-
-    zeros = jnp.zeros(keys.shape, jnp.float32)
-    (key_grad, value_grad), query_grad = lax.scan(
-        backward_block, (zeros, zeros), jnp.arange(blocks)
-    )
-    query_grad = jnp.moveaxis(query_grad, 0, 1).reshape(pairs, tokens, head_dim)
-    image_qkv_grad = (
-        jnp.concatenate([query_grad, key_grad[:, text_len:], value_grad[:, text_len:]], axis=2)
-        .astype(jnp.bfloat16)
-        .reshape(pairs, frame_rows, width, 3 * head_dim)
-    )
-    text_kv_grad = jnp.concatenate(
-        [key_grad[:, :text_len], value_grad[:, :text_len]], axis=2
-    ).astype(jnp.bfloat16)
-    qkv_back, text_back = (
-        lax.all_to_all(image_qkv_grad, "rows", split_axis=1, concat_axis=0, tiled=True),
-        lax.all_to_all(text_kv_grad, "rows", split_axis=1, concat_axis=0, tiled=True),
-    )
-    qkv_back = qkv_back.reshape(images, HEADS, rows_dev, width, 3 * head_dim)
-    text_back = text_back.reshape(images, HEADS, text.shape[1], 2 * head_dim)
     attention_gradient = jnp.einsum(
-        "ihrwk,chk->irwc", qkv_back, qkv_shaped, preferred_element_type=jnp.float32
-    )
+        "ihkp,chk->ipc", qkv_back, qkv_shaped, preferred_element_type=jnp.float32
+    ).reshape(image.shape)
     qkv_grad = jnp.einsum(
-        "irwc,ihrwk->chk", attention_input, qkv_back, preferred_element_type=jnp.float32
-    ).reshape(channels, 3 * channels)
+        "ihkp,ipc->hkc", qkv_back, attn_flat, preferred_element_type=jnp.float32
+    ).reshape(3 * channels, channels)
     text_grad = jnp.einsum(
-        "ihtk,chk->itc", text_back, text_shaped, preferred_element_type=jnp.float32
+        "ihkt,chk->itc", own_text, text_shaped, preferred_element_type=jnp.float32
     )
     text_w_grad = jnp.einsum(
-        "itc,ihtk->chk", text, text_back, preferred_element_type=jnp.float32
-    ).reshape(text_w.shape[0], 2 * channels)
+        "gtc,ghkt->chk", text_cols, text_all, preferred_element_type=jnp.float32
+    ).reshape(text_share, 2 * channels)
     attn_term, attn_gain_grad = group_norm_backward(
         attention_gradient * image_window,
         attention_normalized_input,
@@ -373,7 +475,10 @@
         embed_low, lax.axis_index("rows") * embed_share, embed_share, 1
     )
     embed_w_grad = jnp.einsum(
-        "ic,ik->ck", embed_rows, grad_shifts, preferred_element_type=jnp.float32
+        "ic,ik->ck",
+        lax.all_gather(embed_rows, "items", axis=0, tiled=True),
+        lax.all_gather(grad_shifts, "items", axis=0, tiled=True),
+        preferred_element_type=jnp.float32,
     )
     grad_conv1 = first_output_gradient.astype(jnp.bfloat16)
     conv1_grad = kernel_grad(hidden_pad, grad_conv1)
@@ -388,26 +493,28 @@
         image_window,
     )
     image_grad = (grad_middle + start_term) * image_window
-    rows_sums = (
-        lax.psum_scatter(norm1_grad, "rows", scatter_dimension=0, tiled=True),
-        lax.psum_scatter(conv1_grad, "rows", scatter_dimension=3, tiled=True),
-        lax.psum_scatter(second_norm_gradient2, "rows", scatter_dimension=0, tiled=True),
-        lax.psum_scatter(conv2_grad, "rows", scatter_dimension=3, tiled=True),
-        lax.psum_scatter(attn_gain_grad, "rows", scatter_dimension=0, tiled=True),
-        lax.psum_scatter(qkv_grad, "rows", scatter_dimension=1, tiled=True),
-        lax.psum_scatter(text_w_grad, "rows", scatter_dimension=0, tiled=True),
-        lax.psum_scatter(proj_grad, "rows", scatter_dimension=1, tiled=True),
-    )
+    gains = lax.psum(jnp.stack([norm1_grad, second_norm_gradient2, attn_gain_grad]), ("items", "rows"))
+    share = channels // parts
+    gains = lax.dynamic_slice_in_dim(gains, lax.axis_index("rows") * share, share, 1)
+
+    def total(values):
+        return lax.psum(
+            lax.psum_scatter(values.astype(BF16), "rows", scatter_dimension=0, tiled=True), "items"
+        ).astype(F32)
+
+    def kernel_total(values):
+        return jnp.transpose(total(values), (1, 2, 0)).reshape(3, 3, channels, share)
+
     summed = (
-        lax.psum(rows_sums[0].astype(jnp.bfloat16), "items").astype(jnp.float32),
-        lax.psum(rows_sums[1].astype(jnp.bfloat16), "items").astype(jnp.float32),
-        lax.psum(embed_w_grad.astype(jnp.bfloat16), "items").astype(jnp.float32),
-        lax.psum(rows_sums[2].astype(jnp.bfloat16), "items").astype(jnp.float32),
-        lax.psum(rows_sums[3].astype(jnp.bfloat16), "items").astype(jnp.float32),
-        lax.psum(rows_sums[4].astype(jnp.bfloat16), "items").astype(jnp.float32),
-        lax.psum(rows_sums[5].astype(jnp.bfloat16), "items").astype(jnp.float32),
-        lax.psum(rows_sums[6].astype(jnp.bfloat16), "items").astype(jnp.float32),
-        lax.psum(rows_sums[7].astype(jnp.bfloat16), "items").astype(jnp.float32),
+        gains[0],
+        kernel_total(conv1_grad),
+        embed_w_grad,
+        gains[1],
+        kernel_total(conv2_grad),
+        gains[2],
+        total(qkv_grad).T,
+        text_w_grad,
+        total(proj_grad).T,
     )
     return (
         output,

time: 1030 us -> 644 us (0.63)
  waiting for transfers between devices: 305 us -> 50.7 us
  matrix products: 285 us -> 101 us
  blocking collectives: 135 us -> 242 us
  other arithmetic: 134 us -> 66.7 us
  Pallas kernels: 0 us -> 62 us
  local copies, waits for them, and re-layouts: 98.1 us -> 61.1 us
  loops' own time: 11.3 us -> 0 us
    dot_general x82 -> x26, matrix products: 254 us -> 44.4 us  [the longest x18 24.5 us: kernel_grad(): jnp.einsum('irwk,irwc->kc', grad_out, shifted, preferred_element_type=jnp...]
    reduce_scatter x5 -> x4, waiting for transfers between devices: 154 us -> 0.08 us  [total(): lax.psum_scatter(values.astype(BF16), 'rows', scatter_dimension=0, tiled=...]
    convert_element_type x23 -> x2, other arithmetic: 94.4 us -> 5.35 us  [the longest x1 4 us: shards(): (attention_normalized_input * attention_norm_gain).astype(jnp.bfloat16)]
    all_gather x0 -> x4, blocking collectives: none -> 70.8 us  [the longest x1 45.7 us: shards(): text_back = lax.all_gather(text_grad_pair, 'rows', axis=0, tiled=True)]
    pallas_call x0 -> x1, Pallas kernels: none -> 62 us  [attention(): pl.pallas_call(functools.partial(attention_kernel, width, step, bq), out_...]
    all_to_all x5, waiting for transfers between devices: 96.4 us -> 46.1 us  [the longest x2 46 us: to_pairs(): lax.all_to_all(values, 'rows', split_axis=0, concat_axis=0, tiled=True)]
    psum x1, waiting for transfers between devices: 51 us -> 3.45 us  [total(): lax.psum(lax.psum_scatter(values.astype(BF16), 'rows', scatter_dimension=...]
    psum x1, blocking collectives: 10.3 us -> 37.1 us  [shards(): lax.psum(jnp.stack([norm1_grad, second_norm_gradient2, attn_gain_grad]),...]
  transfers between devices with their start and end apart: 19 -> 19, of which waited for: 7 -> 4; matrix products, arithmetic and copies ran while one was open for 41% -> 30% of each run, Pallas kernels for 0% -> 0%
where the time goes in v1:
time: 644 us; the launch traced here: 633 us
  blocking collectives  242 us (38%)
  matrix products  101 us (16%)
  other arithmetic  66.7 us (10%)
  Pallas kernels  62 us (10%)
  local copies, waits for them, and re-layouts  61.1 us (9%)
  waiting for transfers between devices  50.7 us (8%)
  starting transfers between devices  31.4 us (5%)
  between operations  18.2 us (3%)
    pallas_call x1, Pallas kernels, attention(): pl.pallas_call(functools.partial(attention_kernel, width, step, bq), out_...  62 us
    psum x3, blocking collectives, group_norm_forward(): lax.psum((jnp.sum(shaped, axis=(1, 2, 4)), jnp.sum(shaped * shaped, axis=...  51 us
    psum x2, blocking collectives, group_norm_backward(): lax.psum((jnp.sum(shaped_grad, axis=(1, 2, 4)), jnp.sum(shaped_grad * res...  47.1 us
    all_to_all x2, waiting for transfers between devices, to_pairs(): lax.all_to_all(values, 'rows', split_axis=0, concat_axis=0, tiled=True)  46 us
    all_gather x1, blocking collectives, shards(): text_back = lax.all_gather(text_grad_pair, 'rows', axis=0, tiled=True)  45.7 us
    conv_general_dilated x4, matrix products, conv_apply(): lax.conv_general_dilated(padded, kernel, (1, 1), ((0, 0), (0, 0)), dimens...  44.2 us
    psum x1, blocking collectives, shards(): lax.psum(jnp.stack([norm1_grad, second_norm_gradient2, attn_gain_grad]),...  37.1 us
    dot_general x18, matrix products, kernel_grad(): jnp.einsum('irwk,irwc->kc', grad_out, shifted, preferred_element_type=jnp...  24.5 us
  transfers between devices with their start and end apart: 19, of which 4 were waited for; matrix products, arithmetic and copies ran while one was open for 30% of the time, Pallas kernels for 0%

profile of v1, /device:TPU:0, one launch (start us, length us, event | category | flops | bytes accessed | tf_op | source)
XLA Modules:
  0.0 633.4 jit_solution(14859541860353841872)
XLA Ops:
  13.7 18.1 %all-reduce.7 = (f32[1,32]{1,0:T(1,128)S(1)}, f32[1,32]{1,0:T(1,128)S(1)}) all-reduce(f32[1,32]{1,0:T(1,128)S(1)} %bitcast.590, f32[1,32]{1,0:T(1,128)S(1)} %bitcast.588), channel_id=1, replica_groups=mesh['items'=4,'rows'=8] {'rows'}, use_global_device_ids=true, to_apply=%region_2.0 | all-reduce | flops 64 | bytes 512 | tf_op jit(solution)/shard_map/psum | solution.py:240
  38.6 2.9 fusion.184
  41.5 2.2 pad_maximum_fusion
  43.7 15.4 %fusion.211 = f32[1,8,64,512]{3,0,2,1:T(1,128)S(1)} fusion(bf16[1,10,64,512]{3,0,2,1:T(2,128)(2,1)S(1)} %pad_maximum_fusion, bf16[3,3,512,512]{3,2,1,0:T(8,128)(2,1)S(1)} %copy-done.42), kind=kOutput, calls=%fused_computation.306 | convolution fusion | flops 2390753280 | bytes 6422528 | tf_op jit(solution)/shard_map/conv_general_dilated | solution.py:205
  59.7 15.3 %all-reduce.6 = (f32[1,32]{1,0:T(1,128)S(1)}, f32[1,32]{1,0:T(1,128)S(1)}) all-reduce(f32[1,32]{1,0:T(1,128)S(1)} %bitcast.594, f32[1,32]{1,0:T(1,128)S(1)} %bitcast.589), channel_id=1, replica_groups=mesh['items'=4,'rows'=8] {'rows'}, use_global_device_ids=true, to_apply=%region_8.9 | all-reduce | flops 64 | bytes 512 | tf_op jit(solution)/shard_map/psum | solution.py:240
  78.5 3.5 fusion.83
  82.0 4.0 all-to-all-start.1
  87.4 18.8 %fusion.21 = f32[1,8,64,512]{3,0,2,1:T(1,128)S(1)} fusion(bf16[3,3,512,512]{3,2,1,0:T(8,128)(2,1)} %param.22, bf16[1,10,64,512]{3,2,1,0:T(8,128)(2,1)S(1)} %pad_maximum_fusion.4), kind=kOutput, calls=%fused_computation.42 | convolution fusion | flops 2390753280 | bytes 6422528 | tf_op jit(solution)/shard_map/conv_general_dilated | solution.py:205
  112.6 17.7 %all-reduce.5 = (f32[1,32]{1,0:T(1,128)}, f32[1,32]{1,0:T(1,128)}) all-reduce(f32[1,32]{1,0:T(1,128)} %bitcast.595, f32[1,32]{1,0:T(1,128)} %bitcast.591), channel_id=1, replica_groups=mesh['items'=4,'rows'=8] {'rows'}, use_global_device_ids=true, to_apply=%region_14.15 | all-reduce | flops 64 | bytes 512 | tf_op jit(solution)/shard_map/psum | solution.py:240
  137.1 4.0 multiply_convert_fusion.3
  143.3 4.3 all-to-all-start.2
  149.8 2.4 fusion.212
  153.6 9.4 %all-to-all-done.2.go_ref = bf16[8,64,512]{2,1,0:T(8,128)(2,1)} async-done(((bf16[8,64,512]{2,1,0:T(8,128)(2,1)}), bf16[8,64,512]{2,1,0:T(8,128)(2,1)}, u32[]{:S(2)}, u32[]{:S(2)}) %all-to-all-start.2) | async-done | bytes 524320 | tf_op jit(solution)/shard_map/all_to_all | solution.py:357
  163.0 4.3 all-to-all-start
  168.4 36.6 %all-to-all-done.qkv_ref = bf16[8,192,512]{2,1,0:T(8,128)(2,1)} async-done(((bf16[8,192,512]{2,1,0:T(8,128)(2,1)}), bf16[8,192,512]{2,1,0:T(8,128)(2,1)}, u32[]{:S(2)}, u32[]{:S(2)}) %all-to-all-start) | async-done | bytes 1572896 | tf_op jit(solution)/shard_map/all_to_all | solution.py:357
  205.1 62.0 %shard_map.237 = (bf16[8,64,512]{2,1,0:T(8,128)(2,1)}, bf16[8,192,512]{2,1,0:T(8,128)(2,1)}, bf16[128,128]{1,0:T(8,128)(2,1)}) custom-call(s32[1,2]{1,0:T(1,128)} %broadcast_multiply_fusion.ext_ref, bf16[8,192,512]{2,1,0:T(8,128)(2,1)} %all-to-all-done.qkv_ref, bf16[128,128]{1,0:T(8,128)(2,1)} %bitcast.29.text_ref, bf16[8,64,512]{2,1,0:T(8,128)(2,1)} %all-to-all-done.2.go_ref), custom_call_target="tpu_custom_call" | custom-call | flops 53150220288 | bytes 4194304 | tf_op jit(solution)/shard_map/pallas_call | solution.py:155
  267.0 19.5 %all_to_all.43 = bf16[8,64,512]{2,1,0:T(8,128)(2,1)} all-to-all(bf16[8,64,512]{2,1,0:T(8,128)(2,1)} %get-tuple-element.16), channel_id=1, replica_groups=mesh['items'=4,'rows'=8] {'rows'}, dimensions={0} | all-to-all | bytes 1048576 | tf_op jit(solution)/shard_map/all_to_all | solution.py:365
  286.5 4.3 all-to-all-start.4
  290.9 45.7 %all-gather = bf16[1024,128]{1,0:T(8,128)(2,1)} all-gather(bf16[128,128]{1,0:T(8,128)(2,1)} %get-tuple-element.18), channel_id=2, replica_groups=mesh['items'=4,'rows'=8] {'rows'}, dimensions={0}, use_global_device_ids=true | all-gather | bytes 294912 | tf_op jit(solution)/shard_map/all_gather | solution.py:406
  336.6 2.6 copy.185
  339.2 2.5 convolution_convert_fusion.1
  341.8 4.4 copy.189
  346.2 4.0 fusion.93
  357.5 16.8 %all-reduce.4 = (f32[1,32]{1,0:T(1,128)}, f32[1,32]{1,0:T(1,128)}) all-reduce(f32[1,32]{1,0:T(1,128)} %bitcast.596, f32[1,32]{1,0:T(1,128)} %bitcast.592), channel_id=1, replica_groups=mesh['items'=4,'rows'=8] {'rows'}, use_global_device_ids=true, to_apply=%region_20.21 | all-reduce | flops 64 | bytes 512 | tf_op jit(solution)/shard_map/psum | solution.py:274
  375.5 3.7 convolution_convert_fusion
  386.3 4.7 multiply_convert_fusion.1
  403.0 9.6 %pad_slice_fusion = (bf16[1,8,64,512]{3,0,2,1:T(2,128)(2,1)}, bf16[1,8,64,512]{3,0,2,1:T(2,128)(2,1)}, bf16[1,8,64,512]{3,0,2,1:T(2,128)(2,1)}, bf16[1,8,64,512]...) fusion(bf16[1,10,64,512]{3,0,2,1:T(2,128)(2,1)} %copy-done.8), kind=kLoop, calls=%fused_computation.295 | loop fusion | bytes 3801088 | tf_op jit(solution)/shard_map/slice | solution.py:220
  415.7 4.1 pad_maximum_fusion.2
  423.2 2.3 reshape.604
  427.4 5.0 convolution_select_fusion.1
  433.2 2.4 multiply_reduce_fusion
  436.0 16.3 %all-reduce.3 = (f32[1,32]{1,0:T(1,128)S(1)}, f32[1,32]{1,0:T(1,128)S(1)}) all-reduce(f32[1,32]{1,0:T(1,128)S(1)} %bitcast.593, f32[1,32]{1,0:T(1,128)S(1)} %bitcast.597), channel_id=1, replica_groups=mesh['items'=4,'rows'=8] {'rows'}, use_global_device_ids=true, to_apply=%region_29.30 | all-reduce | flops 64 | bytes 512 | tf_op jit(solution)/shard_map/psum | solution.py:448
  454.5 2.7 fusion.78
  468.7 12.3 %reduce.53 = bf16[2048,16]{1,0:T(8,128)(2,1)} reduce(bf16[2048,1,16]{2,1,0:T(2,128)(2,1)S(1)} %bitcast.554, bf16[]{:T(256)} %broadcast.287), dimensions={1}, to_apply=%bitcast.515.reduce_sub_computation | reduce | bytes 131074
  481.0 2.2 reshape.674
  483.3 3.4 all-to-all-start.5
  486.7 8.1 %all-gather.2 = bf16[4,1,256]{2,1,0:T(2,128)(2,1)S(1)} all-gather(bf16[1,1,256]{2,1,0:T(2,128)(2,1)S(1)} %dynamic-slice_bitcast_fusion), channel_id=1, replica_groups=mesh['items'=4,'rows'=8] {'items'}, dimensions={0}, use_global_device_ids=true | all-gather | bytes 2560 | tf_op jit(solution)/shard_map/all_gather | solution.py:479
  496.3 9.7 %all_gather.19 = bf16[4,128,256]{2,1,0:T(8,128)(2,1)} all-gather(bf16[1,128,256]{2,1,0:T(8,128)(2,1)S(1)} %bitcast.569), channel_id=1, replica_groups=mesh['items'=4,'rows'=8] {'items'}, dimensions={0}, use_global_device_ids=true | all-gather | bytes 327680 | tf_op jit(solution)/shard_map/all_gather | solution.py:392
  506.1 4.3 fusion.6
  521.9 5.0 convolution_select_fusion
  529.4 30.3 %all-reduce.2 = (f32[1,32]{1,0:T(1,128)S(1)}, f32[1,32]{1,0:T(1,128)S(1)}, bf16[1,512]{1,0:T(2,128)(2,1)S(1)}, bf16[1,512]{1,0:T(2,128)(2,1)S(1)}) all-reduce(f32[1,32]{1,0:T(1,128)S(1)} %bitcast.583, f32[1,32]{1,0:T(1,128)S(1)} %bitcast.584, f32[1,512]{1,0:T(1,128)S(1)} %bitcast.581, ...), channel_id=1, replica_groups=mesh['items'=4,'rows'=8] {'rows'}, use_global_device_ids=true, to_apply=%region_35.36 | all-reduce | flops 1088 | bytes 6656 | tf_op jit(solution)/shard_map/psum | solution.py:274
  560.7 2.3 fusion.95
  564.1 7.4 %all-gather.3 = bf16[4,1,1024]{2,1,0:T(2,128)(2,1)S(1)} all-gather(bf16[1,1,1024]{2,1,0:T(2,128)(2,1)S(1)} %maximum_bitcast_fusion.1), channel_id=1, replica_groups=mesh['items'=4,'rows'=8] {'items'}, dimensions={0}, use_global_device_ids=true | all-gather | bytes 10240 | tf_op jit(solution)/shard_map/all_gather | solution.py:480
  571.5 37.1 %psum.147 = f32[3,512]{1,0:T(4,128)S(1)} all-reduce(f32[3,512]{1,0:T(4,128)S(1)} %pad_maximum_fusion.7), channel_id=1, replica_groups=mesh['items'=4,'rows'=8] {'items','rows'}, use_global_device_ids=true, to_apply=%region_43.44 | all-reduce | flops 1536 | bytes 12288 | tf_op jit(solution)/shard_map/psum | solution.py:496
  610.5 4.0 convolution_multiply_fusion
  614.4 3.4 all-reduce.11.cloned.1.call-done
  621.1 2.2 reshape.587
  623.3 2.2 reshape.599
  (264 shorter events, 110.0 us)
Async XLA Ops:
  8.0 133.2 %copy-start = (bf16[512,512]{1,0:T(8,128)(2,1)S(1)}, bf16[512,512]{1,0:T(8,128)(2,1)}, u32[]{:S(2)}) copy-start(bf16[512,512]{1,0:T(8,128)(2,1)} %param.26) | copy-start | bytes 1572868
  34.7 9.0 %copy-start.42 = (bf16[3,3,512,512]{3,2,1,0:T(8,128)(2,1)S(1)}, bf16[3,3,512,512]{3,2,1,0:T(8,128)(2,1)}, u32[]{:S(2)}) copy-start(bf16[3,3,512,512]{3,2,1,0:T(8,128)(2,1)} %param.19) | copy-start | bytes 14155780
  35.6 5.9 copy-start.2
  35.9 5.6 collective-permute-start
  37.3 4.2 collective-permute-start.1
  41.5 33.9 %copy-start.38 = (f32[1,512]{1,0:T(1,128)}, f32[1,512]{1,0:T(1,128)S(1)}, u32[]{:S(2)}) copy-start(f32[1,512]{1,0:T(1,128)S(1)} %get-tuple-element.149) | copy-start | bytes 6148
  43.7 15.4 %copy-start.8 = (bf16[1,10,64,512]{3,0,2,1:T(2,128)(2,1)}, bf16[1,10,64,512]{3,0,2,1:T(2,128)(2,1)S(1)}, u32[]{:S(2)}) copy-start(bf16[1,10,64,512]{3,0,2,1:T(2,128)(2,1)S(1)} %pad_maximum_fusion) | copy-start | bytes 1966084
  43.7 31.6 %copy-start.36 = (f32[512]{0:T(512)S(1)}, f32[512]{0:T(512)}, u32[]{:S(2)}) copy-start(f32[512]{0:T(512)} %param.21) | copy-start | bytes 6148
  43.7 34.8 %copy-start.27 = (bf16[1,16,2048]{2,1,0:T(8,128)(2,1)S(1)}, bf16[1,16,2048]{2,1,0:T(8,128)(2,1)}, u32[]{:S(2)}) copy-start(bf16[1,16,2048]{2,1,0:T(8,128)(2,1)} %param.16) | copy-start | bytes 196612
  75.9 10.1 %copy-start.13 = (bf16[1,8,64,512]{3,2,1,0:T(8,128)(2,1)}, bf16[1,8,64,512]{3,2,1,0:T(8,128)(2,1)S(1)}, u32[]{:S(2)}) copy-start(bf16[1,8,64,512]{3,2,1,0:T(8,128)(2,1)S(1)} %multiply_convert_fusion.4) | copy-start | bytes 1572868
  75.9 10.1 %collective-permute-start.2 = (bf16[1,1,64,512]{3,2,1,0:T(8,128)(2,1)S(1)}, bf16[1,1,64,512]{3,2,1,0:T(8,128)(2,1)S(1)}, u32[]{:S(2)}, u32[]{:S(2)}) collective-permute-start(bf16[1,1,64,512]{3,2,1,0:T(8,128)(2,1)S(1)} %get-tuple-element.145), channel_id=1, source_target_pairs={{0,1},{1,2},{2,3},{3,4},{4,5},{5,6},{6,7},{8,9},{9,10},{10,11},{11... | collective-permute-start | bytes 196616 | tf_op jit(solution)/shard_map/ppermute | solution.py:193
  77.2 8.8 %collective-permute-start.3 = (bf16[1,1,64,512]{3,2,1,0:T(8,128)(2,1)S(1)}, bf16[1,1,64,512]{3,2,1,0:T(8,128)(2,1)S(1)}, u32[]{:S(2)}, u32[]{:S(2)}) collective-permute-start(bf16[1,1,64,512]{3,2,1,0:T(8,128)(2,1)S(1)} %get-tuple-element.146), channel_id=1, source_target_pairs={{1,0},{2,1},{3,2},{4,3},{5,4},{6,5},{7,6},{9,8},{10,9},{11,10},{12... | collective-permute-start | bytes 196616 | tf_op jit(solution)/shard_map/ppermute | solution.py:194
  82.0 61.3 %all-to-all-start.1 = ((bf16[8,16,128]{2,1,0:T(8,128)(2,1)}), bf16[8,16,128]{2,1,0:T(8,128)(2,1)}, u32[]{:S(2)}, u32[]{:S(2)}) async-start(bf16[8,16,128]{2,1,0:T(8,128)(2,1)} %fusion.83), calls=%async_computation.1 | async-start | bytes 65536 | tf_op jit(solution)/shard_map/all_to_all | solution.py:380
  87.4 18.8 %copy-start.1 = (bf16[1,8,64,512]{3,2,1,0:T(8,128)(2,1)S(1)}, bf16[1,8,64,512]{3,2,1,0:T(8,128)(2,1)}, u32[]{:S(2)}) copy-start(bf16[1,8,64,512]{3,2,1,0:T(8,128)(2,1)} %param.14) | copy-start | bytes 1572868
  143.3 19.7 %all-to-all-start.2 = ((bf16[8,64,512]{2,1,0:T(8,128)(2,1)}), bf16[8,64,512]{2,1,0:T(8,128)(2,1)}, u32[]{:S(2)}, u32[]{:S(2)}) async-start(bf16[8,64,512]{2,1,0:T(8,128)(2,1)} %fusion.79), calls=%async_computation.2 | async-start | bytes 1048576 | tf_op jit(solution)/shard_map/all_to_all | solution.py:357
  163.0 42.1 %all-to-all-start = ((bf16[8,192,512]{2,1,0:T(8,128)(2,1)}), bf16[8,192,512]{2,1,0:T(8,128)(2,1)}, u32[]{:S(2)}, u32[]{:S(2)}) async-start(bf16[8,192,512]{2,1,0:T(8,128)(2,1)} %convert_bitcast_fusion), calls=%async_computation | async-start | bytes 3145728 | tf_op jit(solution)/shard_map/all_to_all | solution.py:357
  286.5 55.3 %all-to-all-start.4 = ((bf16[8,192,512]{2,1,0:T(8,128)(2,1)}), bf16[8,192,512]{2,1,0:T(8,128)(2,1)}, u32[]{:S(2)}, u32[]{:S(2)}) async-start(bf16[8,192,512]{2,1,0:T(8,128)(2,1)} %get-tuple-element.17), calls=%async_computation.4 | async-start | bytes 3145728 | tf_op jit(solution)/shard_map/all_to_all | solution.py:365
  290.8 226.0 %all-gather.6.cloned.1.call-start = ((), (), s32[]{:S(2)}) async-start(), calls=%async_computation.14 | async-start | bytes 1310720 | tf_op jit(solution)/shard_map/all_gather | solution.py:408
  336.6 224.0 %reduce-scatter.11.cloned.1.call-start = ((), (), s32[]{:S(2)}) async-start(), calls=%async_computation.13 | async-start | bytes 589824 | tf_op jit(solution)/shard_map/reduce_scatter | solution.py:502
  341.7 218.8 %reduce-scatter.9.cloned.1.call-start = ((), (), s32[]{:S(2)}) async-start(), calls=%async_computation.12 | async-start | bytes 1769472 | tf_op jit(solution)/shard_map/reduce_scatter | solution.py:502
  346.2 4.9 copy-start.7
  346.2 4.9 copy-start.35
  379.2 181.4 %reduce-scatter.7.cloned.1.call-start = ((), (), s32[]{:S(2)}) async-start(), calls=%async_computation.11 | async-start | bytes 5308416 | tf_op jit(solution)/shard_map/reduce_scatter | solution.py:502
  384.9 6.3 %copy-start.26 = (bf16[1,10,64,512]{3,2,1,0:T(8,128)(2,1)S(1)}, bf16[1,10,64,512]{3,2,1,0:T(8,128)(2,1)}, u32[]{:S(2)}) copy-start(bf16[1,10,64,512]{3,2,1,0:T(8,128)(2,1)} %copy-done.25) | copy-start | bytes 1966084
  386.3 6.2 copy-start.14
  386.3 6.2 copy-start.30
  391.1 2.7 copy-start.5
  402.9 157.7 %reduce-scatter.5.cloned.1.call-start = ((), (), s32[]{:S(2)}) async-start(), calls=%async_computation.10 | async-start | bytes 5308416 | tf_op jit(solution)/shard_map/reduce_scatter | solution.py:502
  403.0 9.6 %copy-start.6 = (bf16[1,8,64,512]{3,0,2,1:T(2,128)(2,1)S(1)}, bf16[1,8,64,512]{3,0,2,1:T(2,128)(2,1)}, u32[]{:S(2)}) copy-start(bf16[1,8,64,512]{3,0,2,1:T(2,128)(2,1)} %copy-done.5) | copy-start | bytes 1572868
  403.0 12.7 %copy-start.3 = (bf16[1,8,64,512]{3,0,2,1:T(2,128)(2,1)S(1)}, bf16[1,8,64,512]{3,0,2,1:T(2,128)(2,1)}, u32[]{:S(2)}) copy-start(bf16[1,8,64,512]{3,0,2,1:T(2,128)(2,1)} %copy-done.2) | copy-start | bytes 1572868
  412.8 7.0 %collective-permute-start.4 = (bf16[1,1,64,512]{3,0,2,1:T(2,128)(2,1)S(1)}, bf16[1,1,64,512]{3,0,2,1:T(2,128)(2,1)S(1)}, u32[]{:S(2)}, u32[]{:S(2)}) collective-permute-start(bf16[1,1,64,512]{3,0,2,1:T(2,128)(2,1)S(1)} %get-tuple-element.139), channel_id=1, source_target_pairs={{0,1},{1,2},{2,3},{3,4},{4,5},{5,6},{6,7},{8,9},{9,10},{10,11},{11... | collective-permute-start | bytes 196616 | tf_op jit(solution)/shard_map/ppermute | solution.py:193
  414.1 5.7 collective-permute-start.5
  422.0 5.4 copy-start.43
  452.7 4.5 copy-start.19
  452.7 5.8 copy-start.24
  454.5 11.6 %copy-start.11 = (bf16[1,8,64,512]{3,2,1,0:T(8,128)(2,1)}, bf16[1,8,64,512]{3,2,1,0:T(8,128)(2,1)S(1)}, u32[]{:S(2)}) copy-start(bf16[1,8,64,512]{3,2,1,0:T(8,128)(2,1)S(1)} %multiply_convert_fusion) | copy-start | bytes 1572868
  457.2 2.6 copy-start.23
  458.5 2.6 copy-start.4
  459.8 2.6 copy-start.22
  467.4 19.3 %copy-start.28 = (bf16[1,2048]{1,0:T(2,128)(2,1)S(1)}, bf16[1,2048]{1,0:T(2,128)(2,1)}, u32[]{:S(2)}) copy-start(bf16[1,2048]{1,0:T(2,128)(2,1)} %param.15) | copy-start | bytes 12292
  467.4 38.6 %copy-start.15 = (bf16[1024,128]{1,0:T(8,128)(2,1)S(1)}, bf16[1024,128]{1,0:T(8,128)(2,1)}, u32[]{:S(2)}) copy-start(bf16[1024,128]{1,0:T(8,128)(2,1)} %all-gather) | copy-start | bytes 786436
  483.3 11.6 %all-to-all-start.5 = ((bf16[8,2,2048]{2,1,0:T(2,128)(2,1)}), bf16[8,2,2048]{2,1,0:T(2,128)(2,1)S(1)}, u32[]{:S(2)}, u32[]{:S(2)}) async-start(bf16[8,2,2048]{2,1,0:T(2,128)(2,1)} %reshape.674), calls=%async_computation.8 | async-start | bytes 131072 | tf_op jit(solution)/shard_map/all_to_all | solution.py:391
  486.6 131.3 %all-reduce.11.cloned.1.call-start = ((), (), s32[]{:S(2)}) async-start(), calls=%async_computation.15 | async-start | bytes 2883584 | tf_op jit(solution)/shard_map/psum | solution.py:501
  510.3 6.6 %copy-start.17 = (bf16[4,128,256]{2,1,0:T(8,128)(2,1)S(1)}, bf16[4,128,256]{2,1,0:T(8,128)(2,1)}, u32[]{:S(2)}) copy-start(bf16[4,128,256]{2,1,0:T(8,128)(2,1)} %all_gather.19) | copy-start | bytes 786436
  513.3 7.5 %copy-start.12 = (bf16[1,8,64,512]{3,2,1,0:T(8,128)(2,1)S(1)}, bf16[1,8,64,512]{3,2,1,0:T(8,128)(2,1)}, u32[]{:S(2)}) copy-start(bf16[1,8,64,512]{3,2,1,0:T(8,128)(2,1)} %copy-done.11) | copy-start | bytes 1572868
  514.3 5.6 collective-permute-start.6
  515.6 5.3 collective-permute-start.7
  560.1 11.4 %copy-start.41 = (f32[512]{0:T(512)S(1)}, f32[512]{0:T(512)}, u32[]{:S(2)}) copy-start(f32[512]{0:T(512)} %get-tuple-element.94) | copy-start | bytes 6148
  (15 other events, 16.9 us)
Sparse Core Ops, SparseCore 0:
  336.7 26.9 all-gather.5
  560.8 57.0 all-reduce.10
Sparse Core Ops, SparseCore 1:
  341.8 31.2 reduce-scatter.10
  379.3 32.1 reduce-scatter.8
  413.8 53.2 reduce-scatter.6
  469.5 54.2 reduce-scatter.4

commit v2 on v1

v2 whole, which is shorter than its diff:
```python
import functools

import jax
import jax.numpy as jnp
from jax import lax
from jax.experimental import pallas as pl
from jax.experimental.pallas import tpu as pltpu
from jax.sharding import PartitionSpec as P

GROUPS = 32
HEADS = 8
F32, BF16 = jnp.float32, jnp.bfloat16
NEG = -1e30


def dot(a, b, ca, cb):
    return lax.dot_general(a, b, (((ca,), (cb,)), ((), ())), preferred_element_type=F32)

def attention_kernel(width, step, bq, ext_ref, qkv_ref, text_ref, go_ref, out_ref, dqkv_ref, dtext_ref,
                     kn, vn, kt, vt, s0, s1, e0, e1, dkt, dvt):
    scores, raised = (s0, s1), (e0, e1)
    chunks, _, span = qkv_ref.shape
    tlen = text_ref.shape[0]
    d = go_ref.shape[1]
    pix = chunks * span
    keys = pix + tlen
    steps = keys // step
    rows_ok, cols_ok = ext_ref[0, 0], ext_ref[0, 1]
    def stage(c, carry):
        base = pl.multiple_of(c * span, span)
        pos = base + lax.broadcasted_iota(jnp.int32, (16, span), 1)
        row = lax.broadcasted_iota(jnp.int32, (16, span), 0)
        ok = (pos // width < rows_ok) & (pos % width < cols_ok)
        extra = jnp.where((row == 0) & jnp.logical_not(ok), NEG, 0.0)
        k = qkv_ref[c, d:2 * d, :]
        v = qkv_ref[c, 2 * d:, :]
        kt[:, pl.ds(base, span)] = k
        vt[:, pl.ds(base, span)] = v
        rest = jnp.zeros((128 - d - 16, span), F32)
        ka = jnp.concatenate([k.astype(F32), extra, rest], axis=0)
        va = jnp.concatenate([v.astype(F32), jnp.where(row < 3, 1.0, 0.0), rest], axis=0)
        kn[pl.ds(base, span), :] = ka.T.astype(BF16)
        vn[pl.ds(base, span), :] = va.T.astype(BF16)
        return carry
    lax.fori_loop(0, chunks, stage, 0)
    tk = text_ref[:, :d].astype(F32)
    tv = text_ref[:, d:].astype(F32)
    kt[:, pix:] = tk.T.astype(BF16)
    vt[:, pix:] = tv.T.astype(BF16)
    lanes = lax.broadcasted_iota(jnp.int32, (tlen, 128 - d), 1)
    kn[pix:, :] = jnp.concatenate([tk, jnp.zeros((tlen, 128 - d), F32)], axis=1).astype(BF16)
    vn[pix:, :] = jnp.concatenate([tv, jnp.where(lanes < 3, 1.0, 0.0)], axis=1).astype(BF16)
    dkt[...] = jnp.zeros_like(dkt)
    dvt[...] = jnp.zeros_like(dvt)

    low_peak = jnp.full((8, bq), -3e38, F32)

    def q_aug(c, half):
        q = qkv_ref[c, :d, half * bq:(half + 1) * bq].astype(F32) * (d ** -0.5)
        r = lax.broadcasted_iota(jnp.int32, (128 - d, bq), 0)
        return jnp.concatenate([q, jnp.where(r == 0, 1.0, 0.0)], axis=0).astype(BF16)

    def run(score, exp, back):
        def body(j, carry):
            pk, total, acc, dq = carry
            at = pl.ds(pl.multiple_of(j * step, step), step)
            if score:
                slot, qa = score
                s = dot(kn[at, :], qa, 1, 0)
                scores[slot][at, :] = s
                pk = jnp.maximum(pk, jnp.max(s.reshape(step // 8, 8, bq), axis=0))
            if exp:
                slot, peak = exp
                e = jnp.exp(scores[slot][at, :] - peak)
                total = total + jnp.sum(e.reshape(step // 8, 8, bq), axis=0)
                low = e.astype(BF16)
                raised[slot][at, :] = low
                acc = acc + dot(vt[:, at], low, 1, 0)
            if back:
                slot, goa, gs, q = back
                dp = dot(vn[at, :], goa, 1, 0)
                e = raised[slot][at, :]
                ds = (e.astype(F32) * dp).astype(BF16)
                dvt[:, at] += dot(gs, e, 1, 1)
                dkt[:, at] += dot(q, ds, 1, 1)
                dq = dq + dot(kt[:, at], ds, 1, 0)
            return pk, total, acc, dq
        init = (low_peak, jnp.zeros((8, bq), F32), jnp.zeros((d, bq), F32), jnp.zeros((d, bq), F32))
        return lax.fori_loop(0, steps, body, init)

    def finish_exp(c, half, total, acc):
        inv = 1.0 / jnp.sum(total, axis=0, keepdims=True)
        o = acc * inv
        cols = slice(half * bq, (half + 1) * bq)
        out_ref[c, :, cols] = o.astype(BF16)
        go = go_ref[c, :, cols].astype(F32)
        nd = -jnp.sum(go * o, axis=0, keepdims=True) * inv
        gs = go * inv
        hi = nd.astype(BF16).astype(F32)
        mid = (nd - hi).astype(BF16).astype(F32)
        lo = nd - hi - mid
        r = lax.broadcasted_iota(jnp.int32, (16, bq), 0)
        extra = jnp.where(r == 0, hi, jnp.where(r == 1, mid, jnp.where(r == 2, lo, 0.0)))
        goa = jnp.concatenate([gs, extra, jnp.zeros((128 - d - 16, bq), F32)], axis=0).astype(BF16)
        return goa

    def put_dq(c, half, dq):
        dqkv_ref[c, :d, half * bq:(half + 1) * bq] = (dq * (d ** -0.5)).astype(BF16)

    def top(pk):
        return jnp.max(pk, axis=0, keepdims=True)

    def q_of(c, half):
        return qkv_ref[c, :d, half * bq:(half + 1) * bq]

    pk, _, _, _ = run((0, q_aug(0, 0)), None, None)
    pk, total, acc, _ = run((1, q_aug(0, 1)), (0, top(pk)), None)
    goa = finish_exp(0, 0, total, acc)

    def two(h, carry):
        pk, goa = carry
        pk2, total, acc, dq = run((0, q_aug(h + 1, 0)), (1, top(pk)), (0, goa, goa[:d], q_of(h, 0)))
        put_dq(h, 0, dq)
        goa = finish_exp(h, 1, total, acc)
        pk3, total, acc, dq = run((1, q_aug(h + 1, 1)), (0, top(pk2)), (1, goa, goa[:d], q_of(h, 1)))
        put_dq(h, 1, dq)
        return pk3, finish_exp(h + 1, 0, total, acc)
    pk, goa = lax.fori_loop(0, chunks - 1, two, (pk, goa))
    last = chunks - 1
    _, total, acc, dq = run(None, (1, top(pk)), (0, goa, goa[:d], q_of(last, 0)))
    put_dq(last, 0, dq)
    goa = finish_exp(last, 1, total, acc)
    _, _, _, dq = run(None, None, (1, goa, goa[:d], q_of(last, 1)))
    put_dq(last, 1, dq)

    def finish(c, carry):
        at = pl.ds(pl.multiple_of(c * span, span), span)
        dqkv_ref[c, d:2 * d, :] = (dkt[:, at] * (d ** -0.5)).astype(BF16)
        dqkv_ref[c, 2 * d:, :] = dvt[:, at].astype(BF16)
        return carry
    lax.fori_loop(0, chunks, finish, 0)
    dtext_ref[:d, :] = (dkt[:, pix:] * (d ** -0.5)).astype(BF16)
    dtext_ref[d:, :] = dvt[:, pix:].astype(BF16)

def attention(ext, qkv, text, go, width):
    chunks, wide, span = qkv.shape
    d = wide // 3
    tlen = text.shape[0]
    keys = chunks * span + tlen
    bq = span // 2
    lanes = keys // 128
    step = 128 * max(n for n in range(1, 12) if lanes % n == 0)
    vm = pl.BlockSpec(memory_space=pltpu.VMEM)
    flops = 2 * 6 * chunks * span * keys * d
    return pl.pallas_call(
        functools.partial(attention_kernel, width, step, bq),
        out_shape=(
            jax.ShapeDtypeStruct(go.shape, BF16),
            jax.ShapeDtypeStruct(qkv.shape, BF16),
            jax.ShapeDtypeStruct((2 * d, tlen), BF16),
        ),
        in_specs=[pl.BlockSpec(memory_space=pltpu.SMEM), vm, vm, vm],
        out_specs=(vm, vm, vm),
        scratch_shapes=[
            pltpu.VMEM((keys, 128), BF16),
            pltpu.VMEM((keys, 128), BF16),
            pltpu.VMEM((d, keys), BF16),
            pltpu.VMEM((d, keys), BF16),
            pltpu.VMEM((keys, bq), F32),
            pltpu.VMEM((keys, bq), F32),
            pltpu.VMEM((keys, bq), BF16),
            pltpu.VMEM((keys, bq), BF16),
            pltpu.VMEM((d, keys), F32),
            pltpu.VMEM((d, keys), F32),
        ],
        compiler_params=pltpu.CompilerParams(vmem_limit_bytes=56 << 20),
        cost_estimate=pl.CostEstimate(
            flops=4 * flops, bytes_accessed=16 * chunks * span * d, transcendentals=chunks * span * keys
        ),
    )(ext, qkv, text, go)


MESH = pl.DeviceIdType.MESH
EPS = 1e-05
WHOLE = pl.BlockSpec(memory_space=pltpu.VMEM)
SCALARS = pl.BlockSpec(memory_space=pltpu.SMEM)
ANYWHERE = pl.BlockSpec(memory_space=pl.ANY)


def exchange_kernel(n, count, *refs):
    stats_ref, rows = refs[0], refs[1 : 1 + count]
    total_ref = refs[1 + count]
    outs = refs[2 + count : 2 + 3 * count]
    slots = refs[2 + 3 * count]
    lands = refs[3 + 3 * count : 3 + 5 * count]
    send, recv, row_send, row_recv = refs[3 + 5 * count :]
    me = lax.axis_index("rows")
    barrier = pltpu.get_barrier_semaphore()

    def greet(k, carry):
        pl.semaphore_signal(
            barrier, inc=1, device_id={"rows": lax.rem(me + k, n)}, device_id_type=MESH
        )
        return carry

    lax.fori_loop(1, n, greet, 0)
    slots[me] = stats_ref[...]
    pl.semaphore_wait(barrier, n - 1)

    def share(k):
        return pltpu.make_async_remote_copy(
            src_ref=stats_ref,
            dst_ref=slots.at[me],
            send_sem=send.at[k],
            recv_sem=recv.at[k],
            device_id={"rows": lax.rem(me + k, n)},
            device_id_type=MESH,
        )

    def start(k, carry):
        share(k).start()
        return carry

    lax.fori_loop(1, n, start, 0)

    def row_copy(j, side):
        last = rows[j].shape[1] - 1
        at = last if side == 0 else 0
        return pltpu.make_async_remote_copy(
            src_ref=rows[j].at[:, at : at + 1],
            dst_ref=lands[2 * j + side],
            send_sem=row_send.at[2 * j + side],
            recv_sem=row_recv.at[2 * j + side],
            device_id={"rows": me + 1 if side == 0 else me - 1},
            device_id_type=MESH,
        )

    for j in range(count):

        @pl.when(me < n - 1)
        def _():
            row_copy(j, 0).start()

        @pl.when(me > 0)
        def _():
            row_copy(j, 1).start()

    def finish(k, carry):
        share(k).wait()
        return carry

    lax.fori_loop(1, n, finish, 0)
    total_ref[...] = lax.fori_loop(1, n, lambda k, s: s + slots[k], slots[0])
    for j in range(count):

        @pl.when(me > 0)
        def _():
            row_copy(j, 0).wait_recv()
            outs[2 * j][...] = lands[2 * j][...]

        @pl.when(me == 0)
        def _():
            outs[2 * j][...] = jnp.zeros_like(outs[2 * j])

        @pl.when(me < n - 1)
        def _():
            row_copy(j, 1).wait_recv()
            outs[2 * j + 1][...] = lands[2 * j + 1][...]
            row_copy(j, 0).wait_send()

        @pl.when(me == n - 1)
        def _():
            outs[2 * j + 1][...] = jnp.zeros_like(outs[2 * j + 1])

        @pl.when(me > 0)
        def _():
            row_copy(j, 1).wait_send()


def exchange(stats, rows, identity):
    n = lax.axis_size("rows")
    edge = []
    for array in rows:
        edge += [jax.ShapeDtypeStruct(array.shape[:1] + (1,) + array.shape[2:], array.dtype)] * 2
    count = len(rows)
    return pl.pallas_call(
        functools.partial(exchange_kernel, n, count),
        out_shape=(jax.ShapeDtypeStruct(stats.shape, F32), *edge),
        in_specs=[WHOLE] + [ANYWHERE] * count,
        out_specs=(WHOLE,) * (1 + 2 * count),
        scratch_shapes=[
            pltpu.VMEM((n,) + stats.shape, F32),
            *[pltpu.VMEM(e.shape, e.dtype) for e in edge],
            pltpu.SemaphoreType.DMA((n,)),
            pltpu.SemaphoreType.DMA((n,)),
            pltpu.SemaphoreType.DMA((max(1, 2 * count),)),
            pltpu.SemaphoreType.DMA((max(1, 2 * count),)),
        ],
        compiler_params=pltpu.CompilerParams(collective_id=identity, has_side_effects=True),
        name=f"exchange{identity}",
    )(stats, *rows)


def group_sums(rows):
    channels = rows.shape[1]
    size = channels // GROUPS
    one = lax.broadcasted_iota(jnp.int32, (channels, channels), 0) // size
    two = lax.broadcasted_iota(jnp.int32, (channels, channels), 1) // size
    same = jnp.where(one == two, 1.0, 0.0).astype(BF16)
    high = rows.astype(BF16)
    rest = rows - high.astype(F32)
    mid = rest.astype(BF16)
    tail = (rest - mid.astype(F32)).astype(BF16)
    return dot(high, same, 1, 0) + dot(mid, same, 1, 0) + dot(tail, same, 1, 0)


def image_count(info, i, channels):
    return (info[i, 0] * info[i, 1]).astype(F32) * (channels // GROUPS)


def norm_of(stats, count):
    sums = group_sums(stats)
    average = sums[0:1] / count
    square = sums[1:2] / count
    return average, lax.rsqrt(square - average * average + EPS)


def means_of(stats, weight, count):
    sums = group_sums(stats * weight)
    return sums[0:1] / count, sums[1:2] / count


def window(info, i, row, shape):
    ok = (row >= 0) & (row < info[i, 0])
    limit = jnp.where(ok, info[i, 1], 0)
    return jnp.where(lax.broadcasted_iota(jnp.int32, shape, 0) < limit, 1.0, 0.0)


def padded_row(center, above, below, i, r):
    if r == 0:
        return above[i, 0]
    if r == center.shape[1] + 1:
        return below[i, 0]
    return center[i, r - 1]


def put_shifted(out, i, r, value):
    width, channels = value.shape
    column = lax.broadcasted_iota(jnp.int32, value.shape, 0)
    left = jnp.where(column == 0, 0.0, pltpu.roll(value, 1, 0))
    right = jnp.where(column == width - 1, 0.0, pltpu.roll(value, width - 1, 0))
    out[i, r, :, :channels] = left.astype(BF16)
    out[i, r, :, channels : 2 * channels] = value.astype(BF16)
    out[i, r, :, 2 * channels :] = right.astype(BF16)


def sigmoid(v):
    return 1.0 / (1.0 + jnp.exp(-v))


def silu_slope(v):
    s = sigmoid(v)
    return s * (1.0 + v * (1.0 - s))


def put_stats(stats_ref, i, first, second):
    channels = first.shape[1]
    one = jnp.sum(first, axis=0, keepdims=True)
    two = jnp.sum(second, axis=0, keepdims=True)
    row = lax.broadcasted_iota(jnp.int32, (8, channels), 0)
    stats_ref[i] = jnp.where(row == 0, one, jnp.where(row == 1, two, 0.0))


def tap_rows(shifted, tap, images, rows_dev, width):
    block = shifted[:, pl.ds(tap, rows_dev)]
    return block.reshape(images * rows_dev * width, shifted.shape[3])


def conv1_kernel(info, image, above, below, stats, gain, weight, first, out_stats, shifted, acc):
    images, rows_dev, width, channels = image.shape
    tap = pl.program_id(0)
    base = info[0, 2]

    @pl.when(tap == 0)
    def _():
        for i in range(images):
            average, inverse = norm_of(stats[i], image_count(info, i, channels))
            for r in range(rows_dev + 2):
                inside = window(info, i, base + r - 1, (width, channels))
                start = padded_row(image, above, below, i, r).astype(F32) * inside
                value = (start - average) * inverse * inside * gain[...]
                put_shifted(shifted, i, r, value * sigmoid(value) * inside)

    part = dot(tap_rows(shifted, tap, images, rows_dev, width), weight[0], 1, 0)

    @pl.when(tap == 0)
    def _():
        acc[...] = part

    @pl.when(tap > 0)
    def _():
        acc[...] += part

    @pl.when(tap == 2)
    def _():
        for i in range(images):
            one = two = jnp.zeros((width, channels), F32)
            for r in range(rows_dev):
                inside = window(info, i, base + r, (width, channels))
                at = (i * rows_dev + r) * width
                value = acc[at : at + width] * inside
                first[i, r] = value
                one = one + value
                two = two + value * value
            put_stats(out_stats, i, one, two)


def moved_of(value, inside, average, inverse, gain, scale, shift):
    normal = (value - average) * inverse * inside
    return normal, normal * gain * (1.0 + scale) + shift


def conv2_kernel(
    info, first, above, below, stats, gain, shifts, image, weight, middle, out_stats, shifted, acc
):
    images, rows_dev, width, channels = first.shape
    tap = pl.program_id(0)
    base = info[0, 2]

    @pl.when(tap == 0)
    def _():
        for i in range(images):
            average, inverse = norm_of(stats[i], image_count(info, i, channels))
            scale, shift = shifts[i : i + 1, :channels], shifts[i : i + 1, channels:]
            for r in range(rows_dev + 2):
                inside = window(info, i, base + r - 1, (width, channels))
                value = padded_row(first, above, below, i, r)
                _, moved = moved_of(value, inside, average, inverse, gain[...], scale, shift)
                put_shifted(shifted, i, r, moved * sigmoid(moved) * inside)

    part = dot(tap_rows(shifted, tap, images, rows_dev, width), weight[0], 1, 0)

    @pl.when(tap == 0)
    def _():
        acc[...] = part

    @pl.when(tap > 0)
    def _():
        acc[...] += part

    @pl.when(tap == 2)
    def _():
        for i in range(images):
            one = two = jnp.zeros((width, channels), F32)
            for r in range(rows_dev):
                inside = window(info, i, base + r, (width, channels))
                at = (i * rows_dev + r) * width
                value = (image[i, r].astype(F32) + acc[at : at + width]) * inside
                middle[i, r] = value
                one = one + value
                two = two + value * value
            put_stats(out_stats, i, one, two)


def dgrad(shifted, tap, weight, images, rows_dev, width):
    channels = weight.shape[2]
    lhs = tap_rows(shifted, tap, images, rows_dev, width)
    part = None
    for b in range(3):
        term = dot(
            lhs[:, b * channels : (b + 1) * channels],
            weight[0, (2 - b) * channels : (3 - b) * channels, :],
            1,
            1,
        )
        part = term if part is None else part + term
    return part


def back2_kernel(
    info, grad, grad_above, grad_below, middle, mid_above, mid_below, cot, cot_above, cot_below,
    mid_stats, grad_stats, attn_gain, first, first_stats, gain, shifts, weight,
    grad_middle, moved_grad, out_stats, shifted, acc,
):
    images, rows_dev, width, channels = first.shape
    tap = pl.program_id(0)
    base = info[0, 2]

    @pl.when(tap == 0)
    def _():
        for i in range(images):
            count = image_count(info, i, channels)
            average, inverse = norm_of(mid_stats[i], count)
            mean, cross = means_of(grad_stats[i], attn_gain[...], count)
            for r in range(rows_dev + 2):
                inside = window(info, i, base + r - 1, (width, channels))
                normal = (padded_row(middle, mid_above, mid_below, i, r) - average) * inverse
                dx = padded_row(grad, grad_above, grad_below, i, r) * attn_gain[...]
                term = (dx - mean - normal * cross) * inverse * inside
                total = padded_row(cot, cot_above, cot_below, i, r).astype(F32) + term
                if 0 < r <= rows_dev:
                    grad_middle[i, r - 1] = total
                put_shifted(shifted, i, r, total * inside)

    part = dgrad(shifted, tap, weight, images, rows_dev, width)

    @pl.when(tap == 0)
    def _():
        acc[...] = part

    @pl.when(tap > 0)
    def _():
        acc[...] += part

    @pl.when(tap == 2)
    def _():
        for i in range(images):
            average, inverse = norm_of(first_stats[i], image_count(info, i, channels))
            scale, shift = shifts[i : i + 1, :channels], shifts[i : i + 1, channels:]
            one = two = jnp.zeros((width, channels), F32)
            for r in range(rows_dev):
                inside = window(info, i, base + r, (width, channels))
                at = (i * rows_dev + r) * width
                normal, moved = moved_of(
                    first[i, r], inside, average, inverse, gain[...], scale, shift
                )
                value = acc[at : at + width] * inside * silu_slope(moved)
                moved_grad[i, r] = value
                one = one + value
                two = two + value * normal
            put_stats(out_stats, i, one, two)


def back1_kernel(
    info, grad, grad_above, grad_below, first, first_above, first_below, first_stats, grad_stats,
    gain, shifts, image, image_stats, first_gain, weight,
    pre_grad, out_stats, shifted, acc,
):
    images, rows_dev, width, channels = first.shape
    tap = pl.program_id(0)
    base = info[0, 2]

    @pl.when(tap == 0)
    def _():
        for i in range(images):
            count = image_count(info, i, channels)
            average, inverse = norm_of(first_stats[i], count)
            factor = gain[...] * (1.0 + shifts[i : i + 1, :channels])
            mean, cross = means_of(grad_stats[i], factor, count)
            for r in range(rows_dev + 2):
                inside = window(info, i, base + r - 1, (width, channels))
                normal = (padded_row(first, first_above, first_below, i, r) - average) * inverse
                dx = padded_row(grad, grad_above, grad_below, i, r) * factor
                put_shifted(shifted, i, r, (dx - mean - normal * cross) * inverse * inside)

    part = dgrad(shifted, tap, weight, images, rows_dev, width)

    @pl.when(tap == 0)
    def _():
        acc[...] = part

    @pl.when(tap > 0)
    def _():
        acc[...] += part

    @pl.when(tap == 2)
    def _():
        for i in range(images):
            average, inverse = norm_of(image_stats[i], image_count(info, i, channels))
            one = two = jnp.zeros((width, channels), F32)
            for r in range(rows_dev):
                inside = window(info, i, base + r, (width, channels))
                at = (i * rows_dev + r) * width
                normal = (image[i, r].astype(F32) - average) * inverse * inside
                slope = silu_slope(normal * first_gain[...])
                value = acc[at : at + width] * inside * slope
                pre_grad[i, r] = value
                one = one + value
                two = two + value * normal
            put_stats(out_stats, i, one, two)


def conv_call(kernel, info, inputs, weight, outs, flipped):
    images, rows_dev, width, channels = outs[0].shape

    def whole(shape):
        return pl.BlockSpec(shape, lambda tap: (0,) * len(shape))

    def tap_of(tap):
        return ((2 - tap) if flipped else tap, 0, 0)

    weight = weight.reshape(3, 3 * channels, channels)
    flops = 2 * 9 * images * rows_dev * width * channels * channels
    moved = sum(a.size * a.dtype.itemsize for a in (*inputs, weight, *outs))
    return pl.pallas_call(
        kernel,
        grid=(3,),
        out_shape=tuple(outs),
        in_specs=[SCALARS]
        + [whole(a.shape) for a in inputs]
        + [pl.BlockSpec((1, 3 * channels, channels), tap_of)],
        out_specs=tuple(whole(o.shape) for o in outs),
        scratch_shapes=[pltpu.VMEM((images * rows_dev * width, channels), F32)],
        compiler_params=pltpu.CompilerParams(vmem_limit_bytes=48 << 20),
        cost_estimate=pl.CostEstimate(flops=flops, bytes_accessed=moved, transcendentals=0),
        name=kernel.__name__,
    )(info, *inputs, weight)


def weight_grad_kernel(grads, shifted, out, turned):
    images, padded, width, wide = shifted.shape
    rows_dev, channels = padded - 2, wide // 3
    pixels = images * rows_dev * width
    tap = pl.program_id(0)

    @pl.when(tap == 0)
    def _():
        center = grads[:, 1 : rows_dev + 1, :, channels : 2 * channels]
        turned[...] = center.reshape(pixels, channels).astype(F32).T.astype(BF16)

    column = pl.multiple_of((tap % 3) * channels, channels)
    rhs = shifted[:, pl.ds(tap // 3, rows_dev), :, pl.ds(column, channels)]
    out[...] = dot(turned[...], rhs.reshape(pixels, channels), 1, 0).astype(BF16)


def weight_grad(grads, shifted):
    images, padded, width, wide = shifted.shape
    channels = wide // 3
    pixels = images * (padded - 2) * width

    def whole(shape):
        return pl.BlockSpec(shape, lambda tap: (0,) * len(shape))

    return pl.pallas_call(
        weight_grad_kernel,
        grid=(9,),
        out_shape=jax.ShapeDtypeStruct((channels, 9 * channels), BF16),
        in_specs=[whole(grads.shape), whole(shifted.shape)],
        out_specs=pl.BlockSpec((channels, channels), lambda tap: (0, tap)),
        scratch_shapes=[pltpu.VMEM((channels, pixels), BF16)],
        compiler_params=pltpu.CompilerParams(vmem_limit_bytes=32 << 20),
        cost_estimate=pl.CostEstimate(
            flops=18 * pixels * channels * channels, bytes_accessed=18 * channels * channels, transcendentals=0
        ),
        name="weight_grad",
    )(grads, shifted)


def project_kernel(info, middle, stats, gain, weight, attn, qkv):
    images, rows_dev, width, channels = middle.shape
    pixels = rows_dev * width
    heads, wide = HEADS, weight.shape[0] // HEADS
    base = info[0, 2]
    for i in range(images):
        average, inverse = norm_of(stats[i], image_count(info, i, channels))
        for r in range(rows_dev):
            inside = window(info, i, base + r, (width, channels))
            value = (middle[i, r] - average) * inverse * inside * gain[...]
            attn[i, r * width : (r + 1) * width] = value.astype(BF16)
        for h in range(heads):
            block = dot(weight[h * wide : (h + 1) * wide], attn[i], 1, 1)
            qkv[i * heads + h] = block.astype(BF16)


def project(info, middle, stats, gain, weight):
    images, rows_dev, width, channels = middle.shape
    pixels = rows_dev * width
    return pl.pallas_call(
        project_kernel,
        out_shape=(
            jax.ShapeDtypeStruct((images, pixels, channels), BF16),
            jax.ShapeDtypeStruct((images * HEADS, weight.shape[0] // HEADS, pixels), BF16),
        ),
        in_specs=[SCALARS, WHOLE, WHOLE, WHOLE, WHOLE],
        out_specs=(WHOLE, WHOLE),
        compiler_params=pltpu.CompilerParams(vmem_limit_bytes=32 << 20),
        name="project",
    )(info, middle, stats, gain, weight)


def unproject_kernel(info, middle, stats, grads, weight, out, out_stats):
    images, rows_dev, width, channels = middle.shape
    wide, pixels = grads.shape[1], grads.shape[2]
    base = info[0, 2]
    for i in range(images):
        average, inverse = norm_of(stats[i], image_count(info, i, channels))
        acc = None
        for h in range(HEADS):
            turned = grads[i * HEADS + h].astype(F32).T.astype(BF16)
            term = dot(turned, weight[h * wide : (h + 1) * wide], 1, 0)
            acc = term if acc is None else acc + term
        one = two = jnp.zeros((width, channels), F32)
        for r in range(rows_dev):
            inside = window(info, i, base + r, (width, channels))
            value = acc[r * width : (r + 1) * width] * inside
            out[i, r] = value
            one = one + value
            two = two + value * ((middle[i, r] - average) * inverse)
        put_stats(out_stats, i, one, two)


def unproject(info, middle, stats, grads, weight):
    images, rows_dev, width, channels = middle.shape
    return pl.pallas_call(
        unproject_kernel,
        out_shape=(
            jax.ShapeDtypeStruct(middle.shape, F32),
            jax.ShapeDtypeStruct(stats.shape, F32),
        ),
        in_specs=[SCALARS, WHOLE, WHOLE, WHOLE, WHOLE],
        out_specs=(WHOLE, WHOLE),
        compiler_params=pltpu.CompilerParams(vmem_limit_bytes=32 << 20),
        name="unproject",
    )(info, middle, stats, grads, weight)


def finish_kernel(info, pre_grad, grad_stats, image, stats, gain, grad_middle, out):
    images, rows_dev, width, channels = image.shape
    base = info[0, 2]
    for i in range(images):
        count = image_count(info, i, channels)
        average, inverse = norm_of(stats[i], count)
        mean, cross = means_of(grad_stats[i], gain[...], count)
        for r in range(rows_dev):
            inside = window(info, i, base + r, (width, channels))
            normal = (image[i, r].astype(F32) - average) * inverse
            term = (pre_grad[i, r] * gain[...] - mean - normal * cross) * inverse
            out[i, r] = (grad_middle[i, r] + term) * inside


def finish(info, pre_grad, grad_stats, image, stats, gain, grad_middle):
    return pl.pallas_call(
        finish_kernel,
        out_shape=jax.ShapeDtypeStruct(image.shape, F32),
        in_specs=[SCALARS] + [WHOLE] * 6,
        out_specs=WHOLE,
        compiler_params=pltpu.CompilerParams(vmem_limit_bytes=32 << 20),
        name="finish",
    )(info, pre_grad, grad_stats, image, stats, gain, grad_middle)


def shards(
    image, embed, text, extent, first_norm_gain1, conv1_w, embed_w, second_norm_gain2, conv2_w,
    attention_norm_gain, qkv_w, text_w, proj_w, cotangent,
):
    images, rows_dev, width, channels = image.shape
    parts = lax.axis_size("rows")
    me = lax.axis_index("rows")
    pairs = images * HEADS // parts
    head_dim = channels // HEADS
    pixels = rows_dev * width
    group = max(1, 512 // pixels)
    span = group * pixels
    chunks = parts // group
    tokens = text.shape[1]
    first_row = jnp.full((images, 1), me * rows_dev, jnp.int32)
    info = jnp.concatenate([extent, first_row], axis=1)
    gain1 = first_norm_gain1.reshape(1, channels)
    gain2 = second_norm_gain2.reshape(1, channels)
    gain3 = attention_norm_gain.reshape(1, channels)
    rowpos = me * rows_dev + jnp.arange(rows_dev, dtype=jnp.int32)
    colpos = jnp.arange(width, dtype=jnp.int32)
    inside = (rowpos[None, :, None] < extent[:, 0, None, None]) & (
        colpos[None, None, :] < extent[:, 1, None, None]
    )
    image_window = inside.astype(F32)[..., None]

    gathered_text = lax.all_gather(text, "rows", axis=1, tiled=True)
    embed_float = embed.astype(F32)
    embed_low = jax.nn.silu(embed_float).astype(BF16)
    shifts = jnp.dot(embed_low, embed_w, preferred_element_type=F32)
    qkv_turned = qkv_w.T
    proj_shaped = proj_w.reshape(HEADS, head_dim, channels)

    start = image.astype(F32) * image_window
    zeros = jnp.zeros((images, 6, channels), F32)
    stats0 = jnp.concatenate(
        [
            jnp.sum(start, axis=(1, 2))[:, None],
            jnp.sum(start * start, axis=(1, 2))[:, None],
            zeros,
        ],
        axis=1,
    )
    stats1, image_above, image_below, cot_above, cot_below = exchange(
        stats0, (image, cotangent), 0
    )
    full = jax.ShapeDtypeStruct(image.shape, F32)
    sums = jax.ShapeDtypeStruct((images, 8, channels), F32)
    padded = jax.ShapeDtypeStruct((images, rows_dev + 2, width, 3 * channels), BF16)
    first, stats, hidden3 = conv_call(
        conv1_kernel,
        info,
        (image, image_above, image_below, stats1, gain1),
        conv1_w,
        (full, sums, padded),
        False,
    )
    stats2, first_above, first_below = exchange(stats, (first,), 1)
    middle, stats, second3 = conv_call(
        conv2_kernel,
        info,
        (first, first_above, first_below, stats2, gain2, shifts, image),
        conv2_w,
        (full, sums, padded),
        False,
    )
    stats3, mid_above, mid_below = exchange(stats, (middle,), 2)
    attn_flat, qkv_pix = project(info, middle, stats3, gain3, qkv_turned)

    def to_pairs(values):
        wide = values.shape[1]
        moved = lax.all_to_all(values, "rows", split_axis=0, concat_axis=0, tiled=True)
        moved = moved.reshape(chunks, group, pairs, wide, pixels)
        return jnp.transpose(moved, (2, 0, 3, 1, 4)).reshape(pairs, chunks, wide, span)

    def from_pairs(values):
        wide = values.shape[2]
        moved = values.reshape(pairs, chunks, wide, group, pixels)
        moved = jnp.transpose(moved, (1, 3, 0, 2, 4)).reshape(parts * pairs, wide, pixels)
        return lax.all_to_all(moved, "rows", split_axis=0, concat_axis=0, tiled=True)

    qkv_pair = to_pairs(qkv_pix)
    grad_proj = (cotangent.astype(F32) * image_window).astype(BF16).reshape(images, pixels, channels)
    grad_heads = jnp.einsum(
        "ipc,hdc->ihdp", grad_proj, proj_shaped, preferred_element_type=F32
    ).astype(BF16)
    grad_pair = to_pairs(grad_heads.reshape(images * HEADS, head_dim, pixels))
    pair_results = []
    for p in range(pairs):
        pair = me * pairs + p
        item, head = pair // HEADS, pair % HEADS
        weight = lax.dynamic_slice_in_dim(text_w, head * 2 * head_dim, 2 * head_dim, 1)
        own = lax.dynamic_index_in_dim(gathered_text, item, 0, False)
        text_pair = jnp.dot(own, weight, preferred_element_type=F32).astype(BF16)
        pair_extent = lax.dynamic_slice_in_dim(extent, item, 1, 0)
        pair_results.append(attention(pair_extent, qkv_pair[p], text_pair, grad_pair[p], width))
    attended, qkv_grad_pair, text_grad_pair = (jnp.stack(r) for r in zip(*pair_results))
    qkv_back = from_pairs(qkv_grad_pair)
    heads_out = from_pairs(attended).reshape(images, HEADS, head_dim, pixels)
    text_back = lax.all_gather(text_grad_pair, "rows", axis=0, tiled=True)
    text_back = text_back.reshape(images, HEADS, 2 * head_dim, parts * tokens)

    attn_grad, stats = unproject(info, middle, stats3, qkv_back, qkv_turned)
    stats4, grad_above, grad_below = exchange(stats, (attn_grad,), 3)
    grad_middle, moved_grad, stats, conv2_grad3 = conv_call(
        back2_kernel,
        info,
        (attn_grad, grad_above, grad_below, middle, mid_above, mid_below, cotangent, cot_above,
         cot_below, stats3, stats4, gain3, first, stats2, gain2, shifts),
        conv2_w,
        (full, full, sums, padded),
        True,
    )
    conv2_grad = weight_grad(conv2_grad3, second3)
    stats5, moved_above, moved_below = exchange(stats, (moved_grad,), 4)
    pre_grad, stats, conv1_grad3 = conv_call(
        back1_kernel,
        info,
        (moved_grad, moved_above, moved_below, first, first_above, first_below, stats2, stats5,
         gain2, shifts, image, stats1, gain1),
        conv1_w,
        (full, sums, padded),
        True,
    )
    conv1_grad = weight_grad(conv1_grad3, hidden3)
    (stats6,) = exchange(stats, (), 5)
    image_grad = finish(info, pre_grad, stats6, image, stats1, gain1, grad_middle)

    projected = jnp.einsum(
        "ihdp,hdc->ipc", heads_out, proj_shaped, preferred_element_type=F32
    ).reshape(image.shape)
    output = (middle + projected * image_window).astype(BF16)
    proj_grad = jnp.einsum(
        "ipc,ihdp->chd", grad_proj, heads_out, preferred_element_type=F32
    ).reshape(channels, channels)
    qkv_grad = jnp.einsum(
        "ihkp,ipc->hkc",
        qkv_back.reshape(images, HEADS, 3 * head_dim, pixels),
        attn_flat,
        preferred_element_type=F32,
    ).reshape(3 * channels, channels)
    own_text = lax.dynamic_slice_in_dim(text_back, me * tokens, tokens, 3)
    text_shaped = text_w.reshape(text_w.shape[0], HEADS, 2 * head_dim)
    text_grad = jnp.einsum("ihkt,chk->itc", own_text, text_shaped, preferred_element_type=F32)
    text_share = text.shape[2] // parts
    text_cols = lax.dynamic_slice_in_dim(gathered_text, me * text_share, text_share, 2)
    text_cols = lax.all_gather(text_cols, "items", axis=0, tiled=True)
    text_all = lax.all_gather(text_back, "items", axis=0, tiled=True)
    text_w_grad = jnp.einsum(
        "gtc,ghkt->chk", text_cols, text_all, preferred_element_type=F32
    ).reshape(text_share, 2 * channels)

    scale_sum = stats5[:, 1] * gain2
    grad_shifts = jnp.concatenate([scale_sum, stats5[:, 0]], axis=1).astype(BF16)
    embed_grad = jnp.einsum(
        "ik,ck->ic", grad_shifts, embed_w, preferred_element_type=F32
    ) * silu_slope(embed_float)
    embed_share = embed_w.shape[0] // parts
    embed_rows = lax.dynamic_slice_in_dim(embed_low, me * embed_share, embed_share, 1)
    embed_w_grad = jnp.einsum(
        "ic,ik->ck",
        lax.all_gather(embed_rows, "items", axis=0, tiled=True),
        lax.all_gather(grad_shifts, "items", axis=0, tiled=True),
        preferred_element_type=F32,
    )
    share = channels // parts
    gains = jnp.stack(
        [
            jnp.sum(stats6[:, 1], axis=0),
            jnp.sum(stats5[:, 1] * (1.0 + shifts[:, :channels]), axis=0),
            jnp.sum(stats4[:, 1], axis=0),
        ]
    )
    gains = lax.dynamic_slice_in_dim(gains, me * share, share, 1)
    gains = lax.psum(gains, "items")

    def total(values):
        return lax.psum(
            lax.psum_scatter(values.astype(BF16), "rows", scatter_dimension=0, tiled=True), "items"
        ).astype(F32)

    def kernel_total(values):
        return total(values).T.reshape(3, 3, channels, share)

    return (
        output,
        image_grad,
        embed_grad,
        text_grad,
        gains[0],
        kernel_total(conv1_grad),
        embed_w_grad,
        gains[1],
        kernel_total(conv2_grad),
        gains[2],
        total(qkv_grad).T,
        text_w_grad,
        total(proj_grad).T,
    )


def solution(mesh):
    in_specs = (
        P("items", "rows", None, None),
        P("items", None),
        P("items", "rows", None),
        P("items", None),
        P(),
        P(),
        P(),
        P(),
        P(),
        P(),
        P(),
        P(),
        P(),
        P("items", "rows", None, None),
    )
    out_specs = (
        P("items", "rows", None, None),
        P("items", "rows", None, None),
        P("items", None),
        P("items", "rows", None),
        P("rows"),
        P(None, None, None, "rows"),
        P("rows", None),
        P("rows"),
        P(None, None, None, "rows"),
        P("rows"),
        P(None, "rows"),
        P("rows", None),
        P(None, "rows"),
    )
    return jax.shard_map(shards, mesh=mesh, in_specs=in_specs, out_specs=out_specs, check_vma=False)
```

time: 644 us -> 597 us (0.927); the launches traced: 633 us -> 594 us
  Pallas kernels: 62 us -> 168 us
  blocking collectives: 242 us -> 156 us
  waiting for transfers between devices: 50.7 us -> 135 us
  matrix products: 101 us -> 27.3 us
  other arithmetic: 66.7 us -> 7.73 us
  starting transfers between devices: 31.4 us -> 15.9 us
  local copies, waits for them, and re-layouts: 61.1 us -> 68 us
    psum x7 -> x1, blocking collectives: 152 us -> 10.3 us  [shards(): gains = lax.psum(gains, 'items')]
    pallas_call x0 -> x15, Pallas kernels: none -> 106 us  [the longest x6 59.2 us: exchange(): pl.pallas_call(functools.partial(exchange_kernel, n, count), out_shape=(j...]
    reduce_scatter x4, waiting for transfers between devices: 0.08 us -> 95.1 us  [total(): lax.psum_scatter(values.astype(BF16), 'rows', scatter_dimension=0, tiled=...]
    all_to_all x2, waiting for transfers between devices: 46 us -> 0.01 us  [to_pairs(): lax.all_to_all(values, 'rows', split_axis=0, concat_axis=0, tiled=True)]
    all_gather x0 -> x1, blocking collectives: none -> 46 us  [shards(): gathered_text = lax.all_gather(text, 'rows', axis=1, tiled=True)]
    conv_general_dilated x4 -> x0, matrix products: 44.2 us -> none  [conv_apply(): lax.conv_general_dilated(padded, kernel, (1, 1), ((0, 0), (0, 0)), dimens...]
    unnamed x101 -> x179, local copies, waits for them, and re-layouts: 16.2 us -> 57.2 us
    psum x1, waiting for transfers between devices: 3.45 us -> 39.5 us  [total(): lax.psum(lax.psum_scatter(values.astype(BF16), 'rows', scatter_dimension=...]
  transfers between devices with their start and end apart: 19 -> 9, of which waited for: 4 -> 4; matrix products, arithmetic and copies ran while one was open for 30% -> 7% of each run, Pallas kernels for 0% -> 18%
where the time goes in v2:
time: 597 us; the launch traced here: 594 us
  Pallas kernels  168 us (28%)
  blocking collectives  156 us (26%)
  waiting for transfers between devices  135 us (23%)
  local copies, waits for them, and re-layouts  68 us (11%)
  matrix products  27.3 us (5%)
  between operations  16.4 us (3%)
  starting transfers between devices  15.9 us (3%)
  other arithmetic  7.73 us (1%)
    reduce_scatter x4, waiting for transfers between devices, total(): lax.psum_scatter(values.astype(BF16), 'rows', scatter_dimension=0, tiled=...  95.1 us
    pallas_call x1, Pallas kernels, attention(): pl.pallas_call(functools.partial(attention_kernel, width, step, bq), out_...  62 us
    pallas_call x6, Pallas kernels, exchange(): pl.pallas_call(functools.partial(exchange_kernel, n, count), out_shape=(j...  59.2 us
    unnamed x179, local copies, waits for them, and re-layouts  57.2 us
    all_gather x1, blocking collectives, shards(): gathered_text = lax.all_gather(text, 'rows', axis=1, tiled=True)  46 us
    all_gather x1, blocking collectives, shards(): text_back = lax.all_gather(text_grad_pair, 'rows', axis=0, tiled=True)  45.7 us
    psum x1, waiting for transfers between devices, total(): lax.psum(lax.psum_scatter(values.astype(BF16), 'rows', scatter_dimension=...  39.5 us
    pallas_call x4, Pallas kernels, conv_call(): pl.pallas_call(kernel, grid=(3,), out_shape=tuple(outs), in_specs=[SCALAR...  29.9 us
  transfers between devices with their start and end apart: 9, of which 4 were waited for; matrix products, arithmetic and copies ran while one was open for 7% of the time, Pallas kernels for 18%

profile of v2, /device:TPU:0, one launch (start us, length us, event | category | flops | bytes accessed | tf_op | source)
XLA Modules:
  0.0 594.0 jit_solution(15328406559474328646)
XLA Ops:
  14.9 6.3 %all-to-all-start.1 = ((bf16[8,64,512]{2,1,0:T(8,128)(2,1)}), bf16[8,64,512]{2,1,0:T(8,128)(2,1)}, u32[]{:S(2)}, u32[]{:S(2)}) async-start(bf16[8,64,512]{2,1,0:T(8,128)(2,1)} %fusion.10), calls=%async_computation.1 | async-start | bytes 1048576 | tf_op jit(solution)/shard_map/all_to_all | solution.py:813
  22.0 17.8 %exchange0.1 = (f32[1,8,512]{2,1,0:T(8,128)}, bf16[1,1,64,512]{3,2,1,0:T(8,128)(2,1)}, bf16[1,1,64,512]{3,2,1,0:T(8,128)(2,1)}, bf16[1,1,64,512]{3,2,1,0:T(8,128)(2,1)}, bf16[1,1,64,512]{3,2,1,0:T(8,128)(2,1)}) custom-call(f32[1,8,512]{2,1,0:T(8,128)} %maximum_maximum_fusion.refs_0_, bf16[1,8,64,512]{3,2,1,0:T(8,128)(2,1)} %image.7, bf16[1,8,64,512]{3,2,1,0:T(8,128)(2,1)} %cot.1), custom_call_target="tpu_custom_call" | custom-call | tf_op jit(solution)/shard_map/exchange0/pallas_call | solution.py:286
  39.9 1.7 copy.44
  44.1 6.2 %conv1_kernel.1 = (f32[1,8,64,512]{3,2,1,0:T(8,128)S(1)}, f32[1,8,512]{2,1,0:T(8,128)S(1)}, bf16[1,10,64,1536]{3,2,1,0:T(8,128)(2,1)S(1)}) custom-call(s32[1,3]{1,0:T(1,128)S(1)} %pad_add_fusion.info, bf16[1,8,64,512]{3,2,1,0:T(8,128)(2,1)S(1)} %copy-done.4, bf16[1,1,64,512]{3,2,1,0:T(8,128)(2,1)S(1)} %copy-done.70, bf16[1,1,64,512]{3,2,1,0:T(8,128)(2,1)S(1)} %copy-done.71, ...), custom_call_target="tpu_custom_call" | custom-call | flops 2415919104 | bytes 8423424 | tf_op jit(solution)/shard_map/conv1_kernel/pallas_call | solution.py:595
  53.1 7.9 %exchange1.1 = (f32[1,8,512]{2,1,0:T(8,128)}, f32[1,1,64,512]{3,2,1,0:T(8,128)}, f32[1,1,64,512]{3,2,1,0:T(8,128)}) custom-call(f32[1,8,512]{2,1,0:T(8,128)} %copy-done.42, f32[1,8,64,512]{3,2,1,0:T(8,128)} %copy-done.9), custom_call_target="tpu_custom_call" | custom-call | tf_op jit(solution)/shard_map/exchange1/pallas_call | solution.py:286
  61.1 2.9 fusion.23.shifts
  64.1 6.4 %conv2_kernel.1 = (f32[1,8,64,512]{3,2,1,0:T(8,128)S(1)}, f32[1,8,512]{2,1,0:T(8,128)S(1)}, bf16[1,10,64,1536]{3,2,1,0:T(8,128)(2,1)S(1)}) custom-call(s32[1,3]{1,0:T(1,128)S(1)} %pad_add_fusion.info, f32[1,8,64,512]{3,2,1,0:T(8,128)S(1)} %copy-done.10, f32[1,1,64,512]{3,2,1,0:T(8,128)S(1)} %copy-done.64, f32[1,1,64,512]{3,2,1,0:T(8,128)S(1)} %copy-done.66, ...), custom_call_target="tpu_custom_call" | custom-call | flops 2415919104 | bytes 9607168 | tf_op jit(solution)/shard_map/conv2_kernel/pallas_call | solution.py:595
  73.3 8.6 %exchange2.1 = (f32[1,8,512]{2,1,0:T(8,128)}, f32[1,1,64,512]{3,2,1,0:T(8,128)}, f32[1,1,64,512]{3,2,1,0:T(8,128)}) custom-call(f32[1,8,512]{2,1,0:T(8,128)} %copy-done.43, f32[1,8,64,512]{3,2,1,0:T(8,128)} %copy-done.1), custom_call_target="tpu_custom_call" | custom-call | tf_op jit(solution)/shard_map/exchange2/pallas_call | solution.py:286
  83.9 2.4 project.1
  88.2 4.9 all-to-all-start
  93.1 46.0 %all_gather.18 = bf16[1,128,2048]{2,1,0:T(8,128)(2,1)S(1)} all-gather(bf16[1,16,2048]{2,1,0:T(8,128)(2,1)S(1)} %copy-done.85), channel_id=1, replica_groups=mesh['items'=4,'rows'=8] {'rows'}, dimensions={1}, use_global_device_ids=true | all-gather | bytes 589824 | tf_op jit(solution)/shard_map/all_gather | solution.py:768
  139.9 2.0 fusion.11.text_ref
  141.9 62.0 %shard_map.237 = (bf16[8,64,512]{2,1,0:T(8,128)(2,1)}, bf16[8,192,512]{2,1,0:T(8,128)(2,1)}, bf16[128,128]{1,0:T(8,128)(2,1)}) custom-call(s32[1,2]{1,0:T(1,128)} %ext_ref, bf16[8,192,512]{2,1,0:T(8,128)(2,1)} %all-to-all-done.qkv_ref, bf16[128,128]{1,0:T(8,128)(2,1)} %fusion.11.text_ref, bf16[8,64,512]{2,1,0:T(8,128)(2,1)} %all-to-all-done.1.go_ref), custom_call_target="tpu_custom_call" | custom-call | flops 53150220288 | bytes 4194304 | tf_op jit(solution)/shard_map/pallas_call | solution.py:155
  203.9 4.4 all-to-all-start.3
  208.4 45.7 %all-gather = bf16[1024,128]{1,0:T(8,128)(2,1)} all-gather(bf16[128,128]{1,0:T(8,128)(2,1)} %get-tuple-element.81), channel_id=2, replica_groups=mesh['items'=4,'rows'=8] {'rows'}, dimensions={0}, use_global_device_ids=true | all-gather | bytes 294912 | tf_op jit(solution)/shard_map/all_gather | solution.py:841
  254.8 2.9 unproject.1
  259.3 8.0 %exchange3.1 = (f32[1,8,512]{2,1,0:T(8,128)}, f32[1,1,64,512]{3,2,1,0:T(8,128)}, f32[1,1,64,512]{3,2,1,0:T(8,128)}) custom-call(f32[1,8,512]{2,1,0:T(8,128)} %copy-done.44, f32[1,8,64,512]{3,2,1,0:T(8,128)} %copy-done.12), custom_call_target="tpu_custom_call" | custom-call | tf_op jit(solution)/shard_map/exchange3/pallas_call | solution.py:286
  275.5 8.9 %back2_kernel.1 = (f32[1,8,64,512]{3,2,1,0:T(8,128)S(1)}, f32[1,8,64,512]{3,2,1,0:T(8,128)S(1)}, f32[1,8,512]{2,1,0:T(8,128)S(1)}, bf16[1,10,64,1536]{3,2,1,0:T(8,128)(2,1)}) custom-call(s32[1,3]{1,0:T(1,128)S(1)} %copy-done.48, f32[1,8,64,512]{3,2,1,0:T(8,128)S(1)} %copy-done.13, f32[1,1,64,512]{3,2,1,0:T(8,128)S(1)} %copy-done.25, ...), custom_call_target="tpu_custom_call" | custom-call | flops 2415919104 | bytes 13180928 | tf_op jit(solution)/shard_map/back2_kernel/pallas_call | solution.py:595
  287.0 9.1 %exchange4.1 = (f32[1,8,512]{2,1,0:T(8,128)}, f32[1,1,64,512]{3,2,1,0:T(8,128)}, f32[1,1,64,512]{3,2,1,0:T(8,128)}) custom-call(f32[1,8,512]{2,1,0:T(8,128)} %copy-done.41, f32[1,8,64,512]{3,2,1,0:T(8,128)} %copy-done.19), custom_call_target="tpu_custom_call" | custom-call | tf_op jit(solution)/shard_map/exchange4/pallas_call | solution.py:286
  305.8 8.4 %back1_kernel.1 = (f32[1,8,64,512]{3,2,1,0:T(8,128)S(1)}, f32[1,8,512]{2,1,0:T(8,128)S(1)}, bf16[1,10,64,1536]{3,2,1,0:T(8,128)(2,1)}) custom-call(s32[1,3]{1,0:T(1,128)S(1)} %copy-done.49, f32[1,8,64,512]{3,2,1,0:T(8,128)S(1)} %copy-done.20, f32[1,1,64,512]{3,2,1,0:T(8,128)S(1)} %copy-done.68, f32[1,1,64,512]{3,2,1,0:T(8,128)S(1)} %copy-done.69, ...), custom_call_target="tpu_custom_call" | custom-call | flops 2415919104 | bytes 10952704 | tf_op jit(solution)/shard_map/back1_kernel/pallas_call | solution.py:595
  315.8 1.5 copy-done.76
  317.3 4.5 weight_grad.2
  321.9 2.2 copy-done.6
  327.2 4.5 weight_grad.3
  331.8 2.2 copy-done.7
  334.1 29.2 %all_to_all.20 = bf16[8,64,512]{2,1,0:T(8,128)(2,1)S(1)} all-to-all(bf16[8,64,512]{2,1,0:T(8,128)(2,1)} %get-tuple-element.62), channel_id=1, replica_groups=mesh['items'=4,'rows'=8] {'rows'}, dimensions={0} | all-to-all | bytes 1048576 | tf_op jit(solution)/shard_map/all_to_all | solution.py:821
  363.2 2.3 convolution_convert_fusion.1
  365.7 3.6 convolution_convert_fusion
  369.5 8.1 %all-gather.2 = bf16[4,1,256]{2,1,0:T(2,128)(2,1)S(1)} all-gather(bf16[1,1,256]{2,1,0:T(2,128)(2,1)S(1)} %fusion.32), channel_id=1, replica_groups=mesh['items'=4,'rows'=8] {'items'}, dimensions={0}, use_global_device_ids=true | all-gather | bytes 2560 | tf_op jit(solution)/shard_map/all_gather | solution.py:903
  378.4 9.9 %all_gather.22 = bf16[4,128,256]{2,1,0:T(8,128)(2,1)} all-gather(bf16[1,128,256]{2,1,0:T(8,128)(2,1)S(1)} %constant_dynamic-slice_fusion), channel_id=1, replica_groups=mesh['items'=4,'rows'=8] {'items'}, dimensions={0}, use_global_device_ids=true | all-gather | bytes 327680 | tf_op jit(solution)/shard_map/all_gather | solution.py:888
  388.3 4.3 fusion.3
  394.1 2.6 fusion.9
  396.7 2.9 fusion.17
  399.5 2.5 copy.52
  403.6 7.8 %exchange5.1.grad_stats = f32[1,8,512]{2,1,0:T(8,128)} custom-call(f32[1,8,512]{2,1,0:T(8,128)} %copy-done.45), custom_call_target="tpu_custom_call" | custom-call | tf_op jit(solution)/shard_map/exchange5/pallas_call | solution.py:286
  412.2 2.4 finish.1
  414.6 2.1 reshape.237
  416.7 31.4 %reduce-scatter.7.cloned.1.call-done = bf16[64,4608]{1,0:T(8,128)(2,1)} async-done(((bf16[512,4608]{1,0:T(8,128)(2,1)}), bf16[64,4608]{1,0:T(8,128)(2,1)}) %reduce-scatter.7.cloned.1.call-update) | async-done | bytes 589840 | tf_op jit(solution)/shard_map/reduce_scatter | solution.py:920
  448.1 2.1 reshape.239
  450.2 29.3 %reduce-scatter.11.cloned.1.call-done = bf16[64,512]{1,0:T(8,128)(2,1)} async-done(((bf16[512,512]{1,0:T(8,128)(2,1)}), bf16[64,512]{1,0:T(8,128)(2,1)}) %reduce-scatter.11.cloned.1.call-update) | async-done | bytes 65552 | tf_op jit(solution)/shard_map/reduce_scatter | solution.py:920
  479.6 34.4 %reduce-scatter.9.cloned.1.call-done = bf16[192,512]{1,0:T(8,128)(2,1)} async-done(((bf16[1536,512]{1,0:T(8,128)(2,1)}), bf16[192,512]{1,0:T(8,128)(2,1)}) %reduce-scatter.9.cloned.1.call-update) | async-done | bytes 196624 | tf_op jit(solution)/shard_map/reduce_scatter | solution.py:920
  515.5 10.3 %psum.35 = f32[3,64]{1,0:T(4,128)S(1)} all-reduce(f32[3,64]{1,0:T(4,128)S(1)} %fusion.26), channel_id=1, replica_groups=mesh['items'=4,'rows'=8] {'items'}, use_global_device_ids=true, to_apply=%region_2.3 | all-reduce | flops 192 | bytes 1536 | tf_op jit(solution)/shard_map/psum | solution.py:916
  525.8 7.2 %all-gather.3 = bf16[4,1,1024]{2,1,0:T(2,128)(2,1)S(1)} all-gather(bf16[1,1,1024]{2,1,0:T(2,128)(2,1)S(1)} %maximum_bitcast_fusion), channel_id=1, replica_groups=mesh['items'=4,'rows'=8] {'items'}, dimensions={0}, use_global_device_ids=true | all-gather | bytes 10240 | tf_op jit(solution)/shard_map/all_gather | solution.py:904
  534.9 4.1 convolution_multiply_fusion
  539.0 39.5 %all-reduce.3.cloned.1.call-done = (bf16[3,3,512,64]{2,1,0,3:T(4,128)(2,1)}, bf16[3,3,512,64]{2,1,0,3:T(4,128)(2,1)}, bf16[512,192]{0,1:T(8,128)(2,1)}, bf16[512,64]{0,1:T(8,128)(2,1)}) async-done(((bf16[3,3,512,64]{2,1,0,3:T(4,128)(2,1)}, bf16[3,3,512,64]{2,1,0,3:T(4,128)(2,1)}, bf16[512,192]{0,1:T(8,128)(2,1)}, bf16[512,64]{0,1:T(8,128)(2,1)}), (bf16[3,3,512,64]{2,1,0,3:T(4,128)(2,1)}, ...) | async-done | bytes 1441808 | tf_op jit(solution)/shard_map/psum | solution.py:919
  580.0 2.3 copy.50
  582.3 1.7 transpose.43
  584.1 2.3 copy.51
  (215 shorter events, 57.8 us)
Async XLA Ops:
  8.0 4.9 copy-start
  12.9 28.7 %copy-start.86 = (s32[1,2]{1,0:T(1,128)S(1)}, s32[1,2]{1,0:T(1,128)}, u32[]{:S(2)}) copy-start(s32[1,2]{1,0:T(1,128)} %ext_ref) | copy-start | bytes 28
  12.9 28.8 %copy-start.4 = (bf16[1,8,64,512]{3,2,1,0:T(8,128)(2,1)S(1)}, bf16[1,8,64,512]{3,2,1,0:T(8,128)(2,1)}, u32[]{:S(2)}) copy-start(bf16[1,8,64,512]{3,2,1,0:T(8,128)(2,1)} %image.7) | copy-start | bytes 1572868
  12.9 28.8 %copy-start.58 = (f32[512]{0:T(512)S(1)}, f32[512]{0:T(512)}, u32[]{:S(2)}) copy-start(f32[512]{0:T(512)} %param.18) | copy-start | bytes 6148
  14.9 73.3 %all-to-all-start.1 = ((bf16[8,64,512]{2,1,0:T(8,128)(2,1)}), bf16[8,64,512]{2,1,0:T(8,128)(2,1)}, u32[]{:S(2)}, u32[]{:S(2)}) async-start(bf16[8,64,512]{2,1,0:T(8,128)(2,1)} %fusion.10), calls=%async_computation.1 | async-start | bytes 1048576 | tf_op jit(solution)/shard_map/all_to_all | solution.py:813
  41.7 40.2 %copy-start.46 = (s32[1,3]{1,0:T(1,128)}, s32[1,3]{1,0:T(1,128)S(1)}, u32[]{:S(2)}) copy-start(s32[1,3]{1,0:T(1,128)S(1)} %pad_add_fusion.info) | copy-start | bytes 40
  44.1 16.9 %copy-start.83 = (bf16[1,2048]{1,0:T(2,128)(2,1)S(1)}, bf16[1,2048]{1,0:T(2,128)(2,1)}, u32[]{:S(2)}) copy-start(bf16[1,2048]{1,0:T(2,128)(2,1)} %param.15) | copy-start | bytes 12292
  53.1 10.9 %copy-start.53 = (f32[512]{0:T(512)S(1)}, f32[512]{0:T(512)}, u32[]{:S(2)}) copy-start(f32[512]{0:T(512)} %param.21) | copy-start | bytes 6148
  61.0 3.0 copy-start.10
  61.0 3.0 copy-start.38
  61.1 3.0 copy-start.64
  61.1 3.0 copy-start.66
  64.0 6.4 %copy-start.30 = (f32[1,1024]{1,0:T(1,128)}, f32[1,1024]{1,0:T(1,128)S(1)}, u32[]{:S(2)}) copy-start(f32[1,1024]{1,0:T(1,128)S(1)} %fusion.23.shifts) | copy-start | bytes 12292
  64.1 17.9 %copy-start.51 = (f32[512]{0:T(512)S(1)}, f32[512]{0:T(512)}, u32[]{:S(2)}) copy-start(f32[512]{0:T(512)} %param.23) | copy-start | bytes 6148
  73.3 19.8 %copy-start.85 = (bf16[1,16,2048]{2,1,0:T(8,128)(2,1)S(1)}, bf16[1,16,2048]{2,1,0:T(8,128)(2,1)}, u32[]{:S(2)}) copy-start(bf16[1,16,2048]{2,1,0:T(8,128)(2,1)} %param.16) | copy-start | bytes 196612
  88.2 53.6 %all-to-all-start = ((bf16[8,192,512]{2,1,0:T(8,128)(2,1)}), bf16[8,192,512]{2,1,0:T(8,128)(2,1)}, u32[]{:S(2)}, u32[]{:S(2)}) async-start(bf16[8,192,512]{2,1,0:T(8,128)(2,1)} %copy-done.14), calls=%async_computation | async-start | bytes 3145728 | tf_op jit(solution)/shard_map/all_to_all | solution.py:813
  141.9 112.2 %copy-start.22 = (f32[1,8,512]{2,1,0:T(8,128)S(1)}, f32[1,8,512]{2,1,0:T(8,128)}, u32[]{:S(2)}) copy-start(f32[1,8,512]{2,1,0:T(8,128)} %get-tuple-element.60.stats.mid_stats) | copy-start | bytes 49156
  203.8 50.3 %copy-start.3 = (f32[1,8,64,512]{3,2,1,0:T(8,128)S(1)}, f32[1,8,64,512]{3,2,1,0:T(8,128)}, u32[]{:S(2)}) copy-start(f32[1,8,64,512]{3,2,1,0:T(8,128)} %copy-done.1) | copy-start | bytes 3145732
  203.8 63.4 %copy-start.23 = (f32[1,1,64,512]{3,2,1,0:T(8,128)S(1)}, f32[1,1,64,512]{3,2,1,0:T(8,128)}, u32[]{:S(2)}) copy-start(f32[1,1,64,512]{3,2,1,0:T(8,128)} %get-tuple-element.68.mid_above) | copy-start | bytes 393220
  203.8 63.4 %copy-start.24 = (f32[1,1,64,512]{3,2,1,0:T(8,128)S(1)}, f32[1,1,64,512]{3,2,1,0:T(8,128)}, u32[]{:S(2)}) copy-start(f32[1,1,64,512]{3,2,1,0:T(8,128)} %get-tuple-element.69.mid_below) | copy-start | bytes 393220
  203.8 63.4 %copy-start.28 = (bf16[1,1,64,512]{3,2,1,0:T(8,128)(2,1)S(1)}, bf16[1,1,64,512]{3,2,1,0:T(8,128)(2,1)}, u32[]{:S(2)}) copy-start(bf16[1,1,64,512]{3,2,1,0:T(8,128)(2,1)} %get-tuple-element.70.cot_above) | copy-start | bytes 196612
  203.9 63.4 %copy-start.29 = (bf16[1,1,64,512]{3,2,1,0:T(8,128)(2,1)S(1)}, bf16[1,1,64,512]{3,2,1,0:T(8,128)(2,1)}, u32[]{:S(2)}) copy-start(bf16[1,1,64,512]{3,2,1,0:T(8,128)(2,1)} %get-tuple-element.71.cot_below) | copy-start | bytes 196612
  203.9 50.2 %all-to-all-start.3 = ((bf16[8,192,512]{2,1,0:T(8,128)(2,1)}), bf16[8,192,512]{2,1,0:T(8,128)(2,1)}, u32[]{:S(2)}, u32[]{:S(2)}) async-start(bf16[8,192,512]{2,1,0:T(8,128)(2,1)} %get-tuple-element.63), calls=%async_computation.3 | async-start | bytes 3145728 | tf_op jit(solution)/shard_map/all_to_all | solution.py:821
  208.3 188.4 %all-gather.6.cloned.1.call-start = ((), (), s32[]{:S(2)}) async-start(), calls=%async_computation.12 | async-start | bytes 1310720 | tf_op jit(solution)/shard_map/all_gather | solution.py:889
  254.0 160.6 %reduce-scatter.5.cloned.1.call-start = ((), (), s32[]{:S(2)}) async-start(), calls=%async_computation.8 | async-start | bytes 5308416 | tf_op jit(solution)/shard_map/reduce_scatter | solution.py:920
  275.5 20.6 %copy-start.5 = (bf16[1,8,64,512]{3,2,1,0:T(8,128)(2,1)S(1)}, bf16[1,8,64,512]{3,2,1,0:T(8,128)(2,1)}, u32[]{:S(2)}) copy-start(bf16[1,8,64,512]{3,2,1,0:T(8,128)(2,1)} %image.7) | copy-start | bytes 1572868
  275.5 20.6 %copy-start.11 = (f32[1,8,64,512]{3,2,1,0:T(8,128)S(1)}, f32[1,8,64,512]{3,2,1,0:T(8,128)}, u32[]{:S(2)}) copy-start(f32[1,8,64,512]{3,2,1,0:T(8,128)} %copy-done.9) | copy-start | bytes 3145732
  305.8 10.0 %copy-start.75 = (bf16[1,10,64,1536]{3,2,1,0:T(8,128)(2,1)S(1)}, bf16[1,10,64,1536]{3,2,1,0:T(8,128)(2,1)}, u32[]{:S(2)}) copy-start(bf16[1,10,64,1536]{3,2,1,0:T(8,128)(2,1)} %copy-done.74) | copy-start | bytes 5898244
  315.8 1.5 copy-start.76
  321.9 2.2 copy-start.6
  324.1 124.0 %reduce-scatter.7.cloned.1.call-start = ((), (), s32[]{:S(2)}) async-start(), calls=%async_computation.9 | async-start | bytes 5308416 | tf_op jit(solution)/shard_map/reduce_scatter | solution.py:920
  324.1 1.5 copy-start.61
  331.8 2.2 copy-start.7
  334.0 31.6 %copy-start.63 = (bf16[1,512,512]{2,1,0:T(8,128)(2,1)S(1)}, bf16[1,512,512]{2,1,0:T(8,128)(2,1)}, u32[]{:S(2)}) copy-start(bf16[1,512,512]{2,1,0:T(8,128)(2,1)} %copy-done.62) | copy-start | bytes 1572868
  334.0 145.5 %reduce-scatter.11.cloned.1.call-start = ((), (), s32[]{:S(2)}) async-start(), calls=%async_computation.11 | async-start | bytes 589824 | tf_op jit(solution)/shard_map/reduce_scatter | solution.py:920
  365.6 148.4 %reduce-scatter.9.cloned.1.call-start = ((), (), s32[]{:S(2)}) async-start(), calls=%async_computation.10 | async-start | bytes 1769472 | tf_op jit(solution)/shard_map/reduce_scatter | solution.py:920
  365.6 3.7 copy-start.84
  365.7 22.6 %copy-start.78 = (bf16[1024,128]{1,0:T(8,128)(2,1)S(1)}, bf16[1024,128]{1,0:T(8,128)(2,1)}, u32[]{:S(2)}) copy-start(bf16[1024,128]{1,0:T(8,128)(2,1)} %all-gather) | copy-start | bytes 786436
  369.3 24.7 %copy-start.82 = (f32[8,64]{1,0:T(8,128)S(1)}, f32[8,64]{1,0:T(8,128)}, u32[]{:S(2)}) copy-start(f32[8,64]{1,0:T(8,128)} %copy-done.81) | copy-start | bytes 6148
  369.3 209.2 %all-reduce.3.cloned.1.call-start = ((), (), s32[]{:S(2)}) async-start(), calls=%async_computation.13 | async-start | bytes 3670016 | tf_op jit(solution)/shard_map/psum | solution.py:919
  392.5 4.2 copy-start.80
  394.1 8.8 %copy-start.56 = (f32[512]{0:T(512)S(1)}, f32[512]{0:T(512)}, u32[]{:S(2)}) copy-start(f32[512]{0:T(512)} %param.21) | copy-start | bytes 6148
  394.1 17.4 %copy-start.16 = (f32[1,8,64,512]{3,2,1,0:T(8,128)S(1)}, f32[1,8,64,512]{3,2,1,0:T(8,128)}, u32[]{:S(2)}) copy-start(f32[1,8,64,512]{3,2,1,0:T(8,128)} %copy-done.15) | copy-start | bytes 3145732
  394.1 17.4 %copy-start.37 = (f32[1,8,512]{2,1,0:T(8,128)S(1)}, f32[1,8,512]{2,1,0:T(8,128)}, u32[]{:S(2)}) copy-start(f32[1,8,512]{2,1,0:T(8,128)} %get-tuple-element.52.stats.image_stats) | copy-start | bytes 49156
  394.1 17.4 %copy-start.50 = (s32[1,3]{1,0:T(1,128)S(1)}, s32[1,3]{1,0:T(1,128)}, u32[]{:S(2)}) copy-start(s32[1,3]{1,0:T(1,128)} %copy-done.46) | copy-start | bytes 40
  394.1 17.4 %copy-start.60 = (f32[512]{0:T(512)S(1)}, f32[512]{0:T(512)}, u32[]{:S(2)}) copy-start(f32[512]{0:T(512)} %param.18) | copy-start | bytes 6148
  396.7 14.8 %copy-start.18 = (f32[1,8,64,512]{3,2,1,0:T(8,128)S(1)}, f32[1,8,64,512]{3,2,1,0:T(8,128)}, u32[]{:S(2)}) copy-start(f32[1,8,64,512]{3,2,1,0:T(8,128)} %copy-done.17) | copy-start | bytes 3145732
  402.1 111.9 %copy-start.33 = (f32[1,1024]{1,0:T(1,128)S(1)}, f32[1,1024]{1,0:T(1,128)}, u32[]{:S(2)}) copy-start(f32[1,1024]{1,0:T(1,128)} %copy-done.30) | copy-start | bytes 12292
  (48 other events, 40.8 us)
Sparse Core Ops, SparseCore 0:
  254.2 26.9 all-gather.5
  514.1 64.3 all-reduce.2
Sparse Core Ops, SparseCore 1:
  324.2 64.4 reduce-scatter.4
  390.8 57.2 reduce-scatter.6
  450.2 29.3 reduce-scatter.10
  482.0 31.9 reduce-scatter.8
